TPU v7x, 32 devices: a whole 2x2x4 slice. The times are simulated.
32 devices in a mesh: groups: 2 (over y), tm: 4 (over z), space: 4 (over x, core).
Axes of the slice: x: 2, y: 2, z: 4, core: 2. Of those that a mesh axis runs over, the one named last changes fastest.
Arguments:
- start_noise: float32 [16, 128, 128], P(None, ('groups', 'space')), parts along dimension 1, may hold values from -6 to 6
- time_embed: float32 [4, 128], P('tm'), may hold values from -6 to 6
- keep_rate: float32 [4], P('tm'), may hold values from -0.75 to -0.5, as said below
- denoise_rate: float32 [4], P('tm'), may hold values from 0.125 to 0.375, as said below
- conv_first: bfloat16 [9, 128, 16], replicated, may hold values from -1 to 1
- conv_middle: bfloat16 [9, 128, 128], replicated, may hold values from -0.25 to 0.25
- conv_last: bfloat16 [9, 16, 128], replicated, may hold values from -0.1875 to 0.1875
- out_bias: float32 [16], replicated, may hold values from -3 to 3
Outputs:
- trajectory: float32 [4, 16, 128, 128], P('tm', None, ('groups', 'space')), parts along dimension 2
There are 2 independent parts, one for each index of `groups`. A program takes and returns all parts, laid end to end along the dimension named above; an argument that names none is the same for every part. Nothing has to cross between parts.
Inputs may be any that keep to these rules, and one draw needn't show every extreme that they name: `keep_rate`: every entry times 4 lies between -3 and -2. `denoise_rate`: every entry times 4 lies between 0.5 and 1.5.
All inputs are finite; a program needn't handle non-finite values.
Results may differ from a plain program's by a relative error of at most 0.0031.
Values may be sent and summed in bfloat16 or wider, within the bound.
No kernel may reach another device: no remote copies, remote signals or barrier semaphores. Data moves between devices by JAX's collectives and lax.ppermute only.
A program may use at most 64 MiB of HBM per device.

v0:
```python
import jax
import jax.numpy as jnp
from jax import lax
from jax.sharding import PartitionSpec as P

ITERS = 3


def padded(value, sides, width):
    for axis, dim in sides:
        count, length = (lax.axis_size(axis), value.shape[dim])
        up = [(i, (i + 1) % count) for i in range(count - 1)]
        down = [(j, i) for i, j in up]
        last = lax.slice_in_dim(value, length - width, length, axis=dim)
        initial = lax.slice_in_dim(value, 0, width, axis=dim)
        before = lax.ppermute(last, axis, up)
        after = lax.ppermute(initial, axis, down)
        value = jnp.concatenate([before, value, after], axis=dim)
    return value


def carried_in(part, axis, combine, identity):
    place = lax.axis_index(axis)
    gathered = lax.all_gather(part, axis)
    state = jnp.zeros_like(part) + jnp.asarray(identity, part.dtype)

    def one(turn, state):
        return combine(state, lax.dynamic_index_in_dim(gathered, turn, 0, False))

    return lax.fori_loop(0, place, one, state)


def convolve(field, taps):
    kernel = taps.reshape((3, 3, taps.shape[1], taps.shape[2]))
    result = lax.conv_general_dilated(
        field[None],
        kernel,
        (1, 1),
        ((0, 0), (1, 1)),
        dimension_numbers=("NCHW", "HWOI", "NCHW"),
        preferred_element_type=jnp.float32,
    )
    return result[0]


def inside_rows(margin, count, tile_rows):
    glob_row = lax.axis_index("space") * tile_rows - margin + jnp.arange(count, dtype=jnp.int32)
    valid = (glob_row >= 0) & (glob_row < tile_rows * lax.axis_size("space"))
    return valid.astype(jnp.float32)[None, :, None]


def on_device(
    start_noise, time_embed, keep_rate, denoise_rate, conv_first, conv_middle, conv_last, out_bias
):
    tile_rows = start_noise.shape[1]
    embed = time_embed[0][:, None, None]
    keep = keep_rate[0]
    rate = denoise_rate[0]
    bias = out_bias[:, None, None]
    state = start_noise
    for step in range(ITERS):
        inputs = state.astype(jnp.bfloat16)
        extended = padded(inputs, (("space", 1),), 3)
        first = jax.nn.silu(convolve(extended, conv_first) + embed)
        first = (first * inside_rows(2, tile_rows + 4, tile_rows)).astype(jnp.bfloat16)
        second = jax.nn.silu(convolve(first, conv_middle))
        second = (second * inside_rows(1, tile_rows + 2, tile_rows)).astype(jnp.bfloat16)
        last = convolve(second, conv_last)
        denoised = state + last + bias
        drift = keep * state + rate * denoised
        earlier = carried_in(
            drift, "tm", lambda before, after: before + after, jnp.zeros_like(drift)
        )
        state = start_noise + earlier
    return state[None]


def solution(mesh):
    placed = (
        P(None, ("groups", "space"), None),
        P("tm", None),
        P("tm"),
        P("tm"),
        P(),
        P(),
        P(),
        P(),
    )
    return jax.shard_map(
        on_device,
        mesh=mesh,
        in_specs=placed,
        out_specs=P("tm", None, ("groups", "space"), None),
        check_vma=False,
    )
```

profile of v0, /device:TPU:1, one launch (start us, length us, event | category | flops | bytes accessed | tf_op | source)
XLA Modules:
  0.0 95.6 jit_solution(12822117978748864473)
XLA Ops:
  0.0 1.0 %convert_element_type.51 = bf16[16,16,128]{2,1,0:T(8,128)(2,1)S(1)} convert(f32[16,16,128]{2,1,0:T(8,128)} %param.14) | non-fusion elementwise | flops 32768 | bytes 196608 | tf_op jit(solution)/shard_map/convert_element_type | solution.py:62
  1.0 4.5 %collective-permute-start = (bf16[16,3,128]{2,1,0:T(4,128)(2,1)S(1)}, bf16[16,3,128]{2,1,0:T(4,128)(2,1)S(1)}, u32[]{:S(2)}, u32[]{:S(2)}) collective-permute-start(bf16[16,3,128]{2,1,0:T(4,128)(2,1)S(1)} %get-tuple-element.129), channel_id=1, source_target_pairs={{0,1},{1,2},{2,3},{4,5},{5,6},{6,7},{8,9},{9,10},{10,11},{12,13},{... | collective-permute-start | bytes 36872 | tf_op jit(solution)/shard_map/ppermute | solution.py:16
  5.5 1.9 %collective-permute-start.1 = (bf16[16,3,128]{2,1,0:T(4,128)(2,1)S(1)}, bf16[16,3,128]{2,1,0:T(4,128)(2,1)S(1)}, u32[]{:S(2)}, u32[]{:S(2)}) collective-permute-start(bf16[16,3,128]{2,1,0:T(4,128)(2,1)S(1)} %get-tuple-element.130), channel_id=1, source_target_pairs={{1,0},{2,1},{3,2},{5,4},{6,5},{7,6},{9,8},{10,9},{11,10},{13,12},{... | collective-permute-start | bytes 36872 | tf_op jit(solution)/shard_map/ppermute | solution.py:17
  8.8 1.8 %collective-permute-done.1 = bf16[16,3,128]{2,1,0:T(4,128)(2,1)S(1)} collective-permute-done((bf16[16,3,128]{2,1,0:T(4,128)(2,1)S(1)}, bf16[16,3,128]{2,1,0:T(4,128)(2,1)S(1)}, u32[]{:S(2)}, u32[]{:S(2)}) %collective-permute-start.1) | collective-permute-done | bytes 12320 | tf_op jit(solution)/shard_map/ppermute | solution.py:17
  10.6 0.1 pad
  10.7 0.0 copy-start.3
  10.8 0.0 copy-start.5
  10.8 0.0 copy-start.6
  10.8 0.5 reshape.93
  11.3 1.3 %copy.12 = bf16[16,22,1,8,17]{0,3,4,1,2:T(8,128)(2,1)S(1)} copy(bf16[16,22,1,8,17]{4,3,1,0,2:T(8,128)(2,1)S(1)} %reshape.93) | data formatting | bytes 191488 | tf_op jit(solution)/shard_map/conv_general_dilated | solution.py:35
  12.7 1.6 %fusion.19 = bf16[20,1,8,17,128]{4,2,3,0,1:T(8,128)(2,1)S(1)} fusion(bf16[3,3,128,16]{2,3,1,0:T(8,128)(2,1)S(1)} %bitcast.171, bf16[16,22,1,7,2]{0,3,4,1,2:T(8,128)(2,1)S(1)} %slice.44, bf16[16,22,1,8,17]{0,3,4,1,2:T(8,128)(2,1)S(1)} %copy.12, f32[20]{0:T(128)S(1)} %and_convert_fusion.1, f32[128]{0:T(128)S(1)} %bitcast.177, pred[8,17]{0,1:T(8,128)(4,1)S(1)} %copy-done.6), kind=kOutput, calls=%fused_computation.39 | convolution fusion | flops 103724544 | bytes 839512 | tf_op jit(solution)/shard_map/conv_general_dilated | solution.py:35
  14.3 1.7 %fusion.96 = bf16[18,1,8,17,128]{4,2,3,0,1:T(8,128)(2,1)S(1)} fusion(bf16[3,3,128,128]{3,2,1,0:T(8,128)(2,1)S(1)} %bitcast.165, bf16[20,1,7,1,128]{4,2,3,0,1:T(8,128)(2,1)S(1)} %get-tuple-element.118, bf16[20,1,7,1,128]{4,2,3,0,1:T(8,128)(2,1)S(1)} %get-tuple-element.117, bf16[20,1,8,17,128]{4,2,3,0,1:T(8,128)(2,1)S(1)} %fusion.19, ...), kind=kOutput, calls=%fused_computation.91 | convolution fusion | flops 728029184 | bytes 1689808 | tf_op jit(solution)/shard_map/conv_general_dilated | solution.py:35
  16.1 1.4 %fusion.102 = f32[16,8,17,16]{3,1,2,0:T(8,128)S(1)} fusion(bf16[3,3,16,128]{3,2,1,0:T(8,128)(2,1)S(1)} %bitcast.174, bf16[18,1,7,1,128]{4,2,3,0,1:T(8,128)(2,1)S(1)} %get-tuple-element.124, bf16[18,1,7,1,128]{4,2,3,0,1:T(8,128)(2,1)S(1)} %get-tuple-element.123, bf16[18,1,8,17,128]{4,2,3,0,1:T(8,128)(2,1)S(1)} %fusion.96), kind=kOutput, calls=%fused_computation.95 | convolution fusion | flops 83718144 | bytes 867328 | tf_op jit(solution)/shard_map/conv_general_dilated | solution.py:35
  17.5 0.8 copy.13
  18.3 0.0 copy-start.2
  18.3 0.3 reshape.48
  18.7 0.6 copy-done.1
  19.2 0.1 fusion.152
  19.3 14.4 %all-gather = f32[64,16,128]{2,0,1:T(8,128)S(1)} all-gather(f32[16,16,128]{2,0,1:T(8,128)S(1)} %fusion.152), channel_id=2, replica_groups=mesh['groups'=2,'tm'=4,'space'=4] {'tm'}, dimensions={0}, use_global_device_ids=true | all-gather | bytes 655360 | tf_op jit(solution)/shard_map/all_gather | solution.py:24
  33.8 0.1 fusion.153
  33.9 2.6 %collective-permute-start.2 = (bf16[16,3,128]{2,0,1:T(8,128)(2,1)S(1)}, bf16[16,3,128]{2,0,1:T(8,128)(2,1)S(1)}, u32[]{:S(2)}, u32[]{:S(2)}) collective-permute-start(bf16[16,3,128]{2,0,1:T(8,128)(2,1)S(1)} %get-tuple-element.127), channel_id=1, source_target_pairs={{0,1},{1,2},{2,3},{4,5},{5,6},{6,7},{8,9},{9,10},{10,11},{12,13},{... | collective-permute-start | bytes 36872 | tf_op jit(solution)/shard_map/ppermute | solution.py:16
  36.5 2.1 %collective-permute-start.3 = (bf16[16,3,128]{2,0,1:T(8,128)(2,1)S(1)}, bf16[16,3,128]{2,0,1:T(8,128)(2,1)S(1)}, u32[]{:S(2)}, u32[]{:S(2)}) collective-permute-start(bf16[16,3,128]{2,0,1:T(8,128)(2,1)S(1)} %get-tuple-element.128), channel_id=1, source_target_pairs={{1,0},{2,1},{3,2},{5,4},{6,5},{7,6},{9,8},{10,9},{11,10},{13,12},{... | collective-permute-start | bytes 36872 | tf_op jit(solution)/shard_map/ppermute | solution.py:17
  38.6 2.9 %collective-permute-done.3 = bf16[16,3,128]{2,0,1:T(8,128)(2,1)S(1)} collective-permute-done((bf16[16,3,128]{2,0,1:T(8,128)(2,1)S(1)}, bf16[16,3,128]{2,0,1:T(8,128)(2,1)S(1)}, u32[]{:S(2)}, u32[]{:S(2)}) %collective-permute-start.3) | collective-permute-done | bytes 12320 | tf_op jit(solution)/shard_map/ppermute | solution.py:17
  41.5 0.1 pad.6
  41.7 0.5 reshape.51
  42.2 1.2 %copy.19 = bf16[16,22,1,8,17]{0,3,4,1,2:T(8,128)(2,1)S(1)} copy(bf16[16,22,1,8,17]{4,3,0,1,2:T(8,128)(2,1)S(1)} %reshape.51) | data formatting | bytes 191488 | tf_op jit(solution)/shard_map/conv_general_dilated | solution.py:35
  43.4 1.6 %fusion.21 = bf16[20,1,8,17,128]{4,2,3,0,1:T(8,128)(2,1)S(1)} fusion(bf16[3,3,128,16]{2,3,1,0:T(8,128)(2,1)S(1)} %bitcast.172, bf16[16,22,1,7,2]{0,3,4,1,2:T(8,128)(2,1)S(1)} %slice.52, bf16[16,22,1,8,17]{0,3,4,1,2:T(8,128)(2,1)S(1)} %copy.19, f32[20]{0:T(128)S(1)} %and_convert_fusion.1, f32[128]{0:T(128)S(1)} %bitcast.178, pred[8,17]{0,1:T(8,128)(4,1)S(1)} %copy-done.6), kind=kOutput, calls=%fused_computation.41 | convolution fusion | flops 103724544 | bytes 839512 | tf_op jit(solution)/shard_map/conv_general_dilated | solution.py:35
  45.0 1.7 %fusion.88 = bf16[18,1,8,17,128]{4,2,3,0,1:T(8,128)(2,1)S(1)} fusion(bf16[3,3,128,128]{3,2,1,0:T(8,128)(2,1)S(1)} %bitcast.166, bf16[20,1,7,1,128]{4,2,3,0,1:T(8,128)(2,1)S(1)} %get-tuple-element.116, bf16[20,1,7,1,128]{4,2,3,0,1:T(8,128)(2,1)S(1)} %get-tuple-element.115, bf16[20,1,8,17,128]{4,2,3,0,1:T(8,128)(2,1)S(1)} %fusion.21, ...), kind=kOutput, calls=%fused_computation.89 | convolution fusion | flops 728029184 | bytes 1689808 | tf_op jit(solution)/shard_map/conv_general_dilated | solution.py:35
  46.8 1.4 %fusion.107 = f32[16,8,17,16]{3,1,2,0:T(8,128)S(1)} fusion(bf16[3,3,16,128]{3,2,1,0:T(8,128)(2,1)S(1)} %bitcast.175, bf16[18,1,7,1,128]{4,2,3,0,1:T(8,128)(2,1)S(1)} %get-tuple-element.122, bf16[18,1,7,1,128]{4,2,3,0,1:T(8,128)(2,1)S(1)} %get-tuple-element.121, bf16[18,1,8,17,128]{4,2,3,0,1:T(8,128)(2,1)S(1)} %fusion.88), kind=kOutput, calls=%fused_computation.99 | convolution fusion | flops 83718144 | bytes 867328 | tf_op jit(solution)/shard_map/conv_general_dilated | solution.py:35
  48.3 0.8 copy.20
  49.1 0.3 reshape.61
  49.4 0.1 fusion.148
  49.5 15.1 %all-gather.1 = f32[64,16,128]{2,0,1:T(8,128)S(1)} all-gather(f32[16,16,128]{2,0,1:T(8,128)S(1)} %fusion.148), channel_id=3, replica_groups=mesh['groups'=2,'tm'=4,'space'=4] {'tm'}, dimensions={0}, use_global_device_ids=true | all-gather | bytes 655360 | tf_op jit(solution)/shard_map/all_gather | solution.py:24
  64.6 0.1 fusion.154
  64.7 2.3 %collective-permute-start.4 = (bf16[16,3,128]{2,0,1:T(8,128)(2,1)S(1)}, bf16[16,3,128]{2,0,1:T(8,128)(2,1)S(1)}, u32[]{:S(2)}, u32[]{:S(2)}) collective-permute-start(bf16[16,3,128]{2,0,1:T(8,128)(2,1)S(1)} %get-tuple-element.125), channel_id=1, source_target_pairs={{0,1},{1,2},{2,3},{4,5},{5,6},{6,7},{8,9},{9,10},{10,11},{12,13},{... | collective-permute-start | bytes 36872 | tf_op jit(solution)/shard_map/ppermute | solution.py:16
  67.0 2.2 %collective-permute-start.5 = (bf16[16,3,128]{2,0,1:T(8,128)(2,1)S(1)}, bf16[16,3,128]{2,0,1:T(8,128)(2,1)S(1)}, u32[]{:S(2)}, u32[]{:S(2)}) collective-permute-start(bf16[16,3,128]{2,0,1:T(8,128)(2,1)S(1)} %get-tuple-element.126), channel_id=1, source_target_pairs={{1,0},{2,1},{3,2},{5,4},{6,5},{7,6},{9,8},{10,9},{11,10},{13,12},{... | collective-permute-start | bytes 36872 | tf_op jit(solution)/shard_map/ppermute | solution.py:17
  69.3 2.8 %collective-permute-done.5 = bf16[16,3,128]{2,0,1:T(8,128)(2,1)S(1)} collective-permute-done((bf16[16,3,128]{2,0,1:T(8,128)(2,1)S(1)}, bf16[16,3,128]{2,0,1:T(8,128)(2,1)S(1)}, u32[]{:S(2)}, u32[]{:S(2)}) %collective-permute-start.5) | collective-permute-done | bytes 12320 | tf_op jit(solution)/shard_map/ppermute | solution.py:17
  72.1 0.1 pad.12
  72.2 0.5 reshape.64
  72.7 1.2 %copy.25 = bf16[16,22,1,8,17]{0,3,4,1,2:T(8,128)(2,1)S(1)} copy(bf16[16,22,1,8,17]{4,3,0,1,2:T(8,128)(2,1)S(1)} %reshape.64) | data formatting | bytes 191488 | tf_op jit(solution)/shard_map/conv_general_dilated | solution.py:35
  74.0 1.6 %fusion.23 = bf16[20,1,8,17,128]{4,2,3,0,1:T(8,128)(2,1)S(1)} fusion(bf16[3,3,128,16]{2,3,1,0:T(8,128)(2,1)S(1)} %bitcast.173, bf16[16,22,1,7,2]{0,3,4,1,2:T(8,128)(2,1)S(1)} %slice.60, bf16[16,22,1,8,17]{0,3,4,1,2:T(8,128)(2,1)S(1)} %copy.25, f32[20]{0:T(128)S(1)} %and_convert_fusion.1, f32[128]{0:T(128)S(1)} %bitcast.179, pred[8,17]{0,1:T(8,128)(4,1)S(1)} %copy-done.6), kind=kOutput, calls=%fused_computation.43 | convolution fusion | flops 103724544 | bytes 839512 | tf_op jit(solution)/shard_map/conv_general_dilated | solution.py:35
  75.6 1.7 %fusion.80 = bf16[18,1,8,17,128]{4,2,3,0,1:T(8,128)(2,1)S(1)} fusion(bf16[3,3,128,128]{3,2,1,0:T(8,128)(2,1)S(1)} %bitcast.167, bf16[20,1,7,1,128]{4,2,3,0,1:T(8,128)(2,1)S(1)} %get-tuple-element.114, bf16[20,1,7,1,128]{4,2,3,0,1:T(8,128)(2,1)S(1)} %get-tuple-element.113, bf16[20,1,8,17,128]{4,2,3,0,1:T(8,128)(2,1)S(1)} %fusion.23, ...), kind=kOutput, calls=%fused_computation.87 | convolution fusion | flops 728029184 | bytes 1689808 | tf_op jit(solution)/shard_map/conv_general_dilated | solution.py:35
  77.3 1.4 %fusion.112 = f32[16,8,17,16]{3,1,2,0:T(8,128)S(1)} fusion(bf16[3,3,16,128]{3,2,1,0:T(8,128)(2,1)S(1)} %bitcast.176, bf16[18,1,7,1,128]{4,2,3,0,1:T(8,128)(2,1)S(1)} %get-tuple-element.120, bf16[18,1,7,1,128]{4,2,3,0,1:T(8,128)(2,1)S(1)} %get-tuple-element.119, bf16[18,1,8,17,128]{4,2,3,0,1:T(8,128)(2,1)S(1)} %fusion.80), kind=kOutput, calls=%fused_computation.103 | convolution fusion | flops 83718144 | bytes 867328 | tf_op jit(solution)/shard_map/conv_general_dilated | solution.py:35
  78.8 0.8 copy.26
  79.6 0.3 reshape.74
  79.9 0.1 fusion.144
  80.0 14.9 %all-gather.2 = f32[64,16,128]{2,0,1:T(8,128)S(1)} all-gather(f32[16,16,128]{2,0,1:T(8,128)S(1)} %fusion.144), channel_id=4, replica_groups=mesh['groups'=2,'tm'=4,'space'=4] {'tm'}, dimensions={0}, use_global_device_ids=true | all-gather | bytes 655360 | tf_op jit(solution)/shard_map/all_gather | solution.py:24
  94.9 0.7 add_bitcast_fusion
  (35 shorter events, 0.4 us)
Async XLA Ops:
  0.0 14.2 %copy-start = (bf16[9,128,128]{2,1,0:T(8,128)(2,1)S(1)}, bf16[9,128,128]{2,1,0:T(8,128)(2,1)}, u32[]{:S(2)}) copy-start(bf16[9,128,128]{2,1,0:T(8,128)(2,1)} %param.19) | copy-start | bytes 884740
  1.0 7.8 %collective-permute-start = (bf16[16,3,128]{2,1,0:T(4,128)(2,1)S(1)}, bf16[16,3,128]{2,1,0:T(4,128)(2,1)S(1)}, u32[]{:S(2)}, u32[]{:S(2)}) collective-permute-start(bf16[16,3,128]{2,1,0:T(4,128)(2,1)S(1)} %get-tuple-element.129), channel_id=1, source_target_pairs={{0,1},{1,2},{2,3},{4,5},{5,6},{6,7},{8,9},{9,10},{10,11},{12,13},{... | collective-permute-start | bytes 36872 | tf_op jit(solution)/shard_map/ppermute | solution.py:16
  5.5 5.1 %collective-permute-start.1 = (bf16[16,3,128]{2,1,0:T(4,128)(2,1)S(1)}, bf16[16,3,128]{2,1,0:T(4,128)(2,1)S(1)}, u32[]{:S(2)}, u32[]{:S(2)}) collective-permute-start(bf16[16,3,128]{2,1,0:T(4,128)(2,1)S(1)} %get-tuple-element.130), channel_id=1, source_target_pairs={{1,0},{2,1},{3,2},{5,4},{6,5},{7,6},{9,8},{10,9},{11,10},{13,12},{... | collective-permute-start | bytes 36872 | tf_op jit(solution)/shard_map/ppermute | solution.py:17
  10.7 1.9 %copy-start.3 = (bf16[9,128,16]{1,2,0:T(8,128)(2,1)S(1)}, bf16[9,128,16]{1,2,0:T(8,128)(2,1)}, u32[]{:S(2)}) copy-start(bf16[9,128,16]{1,2,0:T(8,128)(2,1)} %param.18) | copy-start | bytes 110596
  10.8 1.9 %copy-start.5 = (f32[1,128]{1,0:T(1,128)S(1)}, f32[1,128]{1,0:T(1,128)}, u32[]{:S(2)}) copy-start(f32[1,128]{1,0:T(1,128)} %param.15) | copy-start | bytes 1540
  10.8 1.9 %copy-start.6 = (pred[8,17]{0,1:T(8,128)(4,1)S(1)}, pred[8,17]{0,1:T(8,128)(4,1)}, u32[]{:S(2)}) copy-start(pred[8,17]{0,1:T(8,128)(4,1)} %constant.86) | copy-start | bytes 412
  14.3 1.8 %copy-start.4 = (bf16[9,16,128]{2,1,0:T(8,128)(2,1)S(1)}, bf16[9,16,128]{2,1,0:T(8,128)(2,1)}, u32[]{:S(2)}) copy-start(bf16[9,16,128]{2,1,0:T(8,128)(2,1)} %param.20) | copy-start | bytes 110596
  18.3 0.9 copy-start.1
  18.3 0.9 copy-start.2
  33.9 4.8 %collective-permute-start.2 = (bf16[16,3,128]{2,0,1:T(8,128)(2,1)S(1)}, bf16[16,3,128]{2,0,1:T(8,128)(2,1)S(1)}, u32[]{:S(2)}, u32[]{:S(2)}) collective-permute-start(bf16[16,3,128]{2,0,1:T(8,128)(2,1)S(1)} %get-tuple-element.127), channel_id=1, source_target_pairs={{0,1},{1,2},{2,3},{4,5},{5,6},{6,7},{8,9},{9,10},{10,11},{12,13},{... | collective-permute-start | bytes 36872 | tf_op jit(solution)/shard_map/ppermute | solution.py:16
  36.5 5.0 %collective-permute-start.3 = (bf16[16,3,128]{2,0,1:T(8,128)(2,1)S(1)}, bf16[16,3,128]{2,0,1:T(8,128)(2,1)S(1)}, u32[]{:S(2)}, u32[]{:S(2)}) collective-permute-start(bf16[16,3,128]{2,0,1:T(8,128)(2,1)S(1)} %get-tuple-element.128), channel_id=1, source_target_pairs={{1,0},{2,1},{3,2},{5,4},{6,5},{7,6},{9,8},{10,9},{11,10},{13,12},{... | collective-permute-start | bytes 36872 | tf_op jit(solution)/shard_map/ppermute | solution.py:17
  64.7 4.6 %collective-permute-start.4 = (bf16[16,3,128]{2,0,1:T(8,128)(2,1)S(1)}, bf16[16,3,128]{2,0,1:T(8,128)(2,1)S(1)}, u32[]{:S(2)}, u32[]{:S(2)}) collective-permute-start(bf16[16,3,128]{2,0,1:T(8,128)(2,1)S(1)} %get-tuple-element.125), channel_id=1, source_target_pairs={{0,1},{1,2},{2,3},{4,5},{5,6},{6,7},{8,9},{9,10},{10,11},{12,13},{... | collective-permute-start | bytes 36872 | tf_op jit(solution)/shard_map/ppermute | solution.py:16
  67.0 5.0 %collective-permute-start.5 = (bf16[16,3,128]{2,0,1:T(8,128)(2,1)S(1)}, bf16[16,3,128]{2,0,1:T(8,128)(2,1)S(1)}, u32[]{:S(2)}, u32[]{:S(2)}) collective-permute-start(bf16[16,3,128]{2,0,1:T(8,128)(2,1)S(1)} %get-tuple-element.126), channel_id=1, source_target_pairs={{1,0},{2,1},{3,2},{5,4},{6,5},{7,6},{9,8},{10,9},{11,10},{13,12},{... | collective-permute-start | bytes 36872 | tf_op jit(solution)/shard_map/ppermute | solution.py:17
where the time goes:
time: 95.9 us; the launch traced here: 95.6 us
  blocking collectives  44.4 us (46%)
  starting transfers between devices  15.7 us (16%)
  matrix products  14.2 us (15%)
  local copies, waits for them, and re-layouts  9.87 us (10%)
  waiting for transfers between devices  7.45 us (8%)
  other arithmetic  2.16 us (2%)
  between operations  1.79 us (2%)
    all_gather x3, blocking collectives, carried_in(): gathered = lax.all_gather(part, axis)  44.4 us
    conv_general_dilated x9, matrix products, convolve(): lax.conv_general_dilated(field[None], kernel, (1, 1), ((0, 0), (1, 1)), d...  14.2 us
    ppermute x3, starting transfers between devices, padded(): before = lax.ppermute(last, axis, up)  9.46 us
    conv_general_dilated x15, local copies, waits for them, and re-layouts, convolve(): lax.conv_general_dilated(field[None], kernel, (1, 1), ((0, 0), (1, 1)), d...  8.74 us
    ppermute x3, waiting for transfers between devices, padded(): after = lax.ppermute(initial, axis, down)  7.44 us
    ppermute x3, starting transfers between devices, padded(): after = lax.ppermute(initial, axis, down)  6.25 us
  transfers between devices with their start and end apart: 6, of which 3 were waited for; matrix products, arithmetic and copies ran while one was open for 0% of the time, Pallas kernels for 0%

commit v1 on v0

v1 whole, which is shorter than its diff:
```python
import jax
import jax.numpy as jnp
from jax import lax
from jax.experimental import pallas as pl
from jax.experimental.pallas import tpu as pltpu
from jax.sharding import PartitionSpec as P

ITERS = 3
HALO = 3 * ITERS
BF16 = jnp.bfloat16
F32 = jnp.float32


def padded(value, sides, width):
    for axis, dim in sides:
        count, length = (lax.axis_size(axis), value.shape[dim])
        up = [(i, (i + 1) % count) for i in range(count - 1)]
        down = [(j, i) for i, j in up]
        last = lax.slice_in_dim(value, length - width, length, axis=dim)
        initial = lax.slice_in_dim(value, 0, width, axis=dim)
        before = lax.ppermute(last, axis, up)
        after = lax.ppermute(initial, axis, down)
        value = jnp.concatenate([before, value, after], axis=dim)
    return value


def carried_in(part, axis):
    place = lax.axis_index(axis)
    gathered = lax.all_gather(part, axis)
    earlier = jnp.arange(gathered.shape[0]) < place
    return jnp.sum(jnp.where(earlier[:, None, None, None], gathered, 0.0), axis=0)


def convolve(field, taps):
    kernel = taps.reshape((3, 3, taps.shape[1], taps.shape[2]))
    result = lax.conv_general_dilated(
        field[None],
        kernel,
        (1, 1),
        ((0, 0), (1, 1)),
        dimension_numbers=("NCHW", "HWOI", "NCHW"),
        preferred_element_type=F32,
    )
    return result[0]


def inside_rows(margin, count, tile_rows):
    glob_row = lax.axis_index("space") * tile_rows - margin + jnp.arange(count, dtype=jnp.int32)
    valid = (glob_row >= 0) & (glob_row < tile_rows * lax.axis_size("space"))
    return valid.astype(F32)[None, :, None]


def picard(
    start_noise, time_embed, keep_rate, denoise_rate, conv_first, conv_middle, conv_last, out_bias
):
    tile_rows = start_noise.shape[1]
    embed = time_embed[0][:, None, None]
    keep = keep_rate[0]
    rate = denoise_rate[0]
    bias = out_bias[:, None, None]
    state = start_noise
    for step in range(ITERS):
        inputs = state.astype(BF16)
        extended = padded(inputs, (("space", 1),), 3)
        first = jax.nn.silu(convolve(extended, conv_first) + embed)
        first = (first * inside_rows(2, tile_rows + 4, tile_rows)).astype(BF16)
        second = jax.nn.silu(convolve(first, conv_middle))
        second = (second * inside_rows(1, tile_rows + 2, tile_rows)).astype(BF16)
        last = convolve(second, conv_last)
        denoised = state + last + bias
        drift = keep * state + rate * denoised
        state = start_noise + carried_in(drift, "tm")
    return state[None]


COLS = 128
GRAIN = 16
PAD = COLS + 2 * GRAIN


def pack_kernel(noise_ref, embed_ref, keep_ref, rate_ref, up_ref, down_ref, far_ref):
    rows = noise_ref.shape[1]
    params = jnp.concatenate(
        [
            embed_ref[...],
            jnp.full((1, COLS), keep_ref[0], F32),
            jnp.full((1, COLS), rate_ref[0], F32),
            jnp.zeros((5, COLS), F32),
        ],
        axis=0,
    )
    full = jnp.concatenate([params, jnp.zeros((8, COLS), F32)], axis=0)
    for i in range(HALO):
        up_ref[i] = noise_ref[:, rows - HALO + i, :]
        down_ref[i] = noise_ref[:, i, :]
    up_ref[HALO] = full
    down_ref[HALO] = full
    far_ref[...] = params


def weights_kernel(first_ref, middle_ref, last_ref, w1a_ref, w1b_ref, wm_ref, w3_ref):
    w1a_ref[...] = jnp.zeros(w1a_ref.shape, BF16)
    w1b_ref[...] = jnp.zeros(w1b_ref.shape, BF16)
    for tap in range(9):
        a, b = divmod(tap, 3)
        block = (first_ref[tap].astype(F32).T * 0.5).astype(BF16)
        for out in range(6):
            row = out + a
            w1a_ref[pl.ds(128 * b + 16 * row, 16), pl.ds(128 * out, 128)] = block
        for out in range(2):
            row = 6 + out + a
            place = row - 8 if row >= 8 else row
            w1b_ref[pl.ds(128 * b + 16 * place, 16), pl.ds(128 * out, 128)] = block
        block = (middle_ref[tap].astype(F32).T * 0.5).astype(BF16)
        for out in range(2):
            wm_ref[pl.ds(512 * b + 128 * (out + a), 128), pl.ds(128 * out, 128)] = block
    zero = jnp.zeros((128, 128), BF16)
    for b in range(3):
        wm_ref[pl.ds(512 * b + 384, 128), pl.ds(0, 128)] = zero
        wm_ref[pl.ds(512 * b, 128), pl.ds(128, 128)] = zero
        for row in range(10):
            parts = []
            for out in range(8):
                a = row - out
                if 0 <= a < 3:
                    parts.append(last_ref[3 * a + b].astype(F32))
                else:
                    parts.append(jnp.zeros((16, 128), F32))
            block = jnp.concatenate(parts, axis=0).T.astype(BF16)
            w3_ref[pl.ds(128 * row, 128), pl.ds(128 * b, 128)] = block


def split3(value):
    high = value.astype(BF16)
    rest = value - high.astype(F32)
    mid = rest.astype(BF16)
    low = (rest - mid.astype(F32)).astype(BF16)
    return high, mid, low


def shifted_rows(grain, by):
    row = lax.broadcasted_iota(jnp.int32, grain.shape, 0)
    if by > 0:
        return jnp.where(row == 0, 0.0, pltpu.roll(grain, 1, 0))
    return jnp.where(row == GRAIN - 1, 0.0, pltpu.roll(grain, GRAIN - 1, 0))


def half_silu(half):
    return half * jnp.tanh(half) + half


def chain_kernel(
    tm_size,
    space_size,
    rows,
    noise_ref,
    before_ref,
    after_ref,
    far_ref,
    place_ref,
    bias_ref,
    w1a_ref,
    w1b_ref,
    wm_ref,
    w3_ref,
    out_ref,
    state_ref,
    zb_ref,
    first_ref,
    second_ref,
):
    time = place_ref[0]
    tile = place_ref[1]
    top = (tile > 0).astype(F32)
    bottom = (tile < space_size - 1).astype(F32)

    w_new = lax.broadcasted_iota(jnp.int32, (COLS, COLS), 0)
    w_old = lax.broadcasted_iota(jnp.int32, (COLS, COLS), 1)
    order = jnp.where(w_old == (w_new % GRAIN) * 8 + w_new // GRAIN, 1.0, 0.0).astype(BF16)
    lane = lax.broadcasted_iota(jnp.int32, (1, COLS), 1)
    lane_row = lane // 16

    def row_scale(rel):
        if rel < 0:
            return top
        if rel >= rows:
            return bottom
        return None

    def lane_scale(tile_index, halo):
        rel = lane_row + (8 * tile_index - halo)
        return jnp.where(rel < 0, top, jnp.where(rel >= rows, bottom, 1.0))

    total = rows + 2 * HALO
    for t in range(pl.cdiv(total, 8)):
        parts = []
        for e in range(8 * t, 8 * t + 8):
            if e < HALO:
                parts.append(before_ref[e])
            elif e < HALO + rows:
                parts.append(noise_ref[:, e - HALO, :])
            elif e < total:
                parts.append(after_ref[e - HALO - rows])
            else:
                parts.append(jnp.zeros((16, COLS), F32))
        block = jnp.concatenate(parts, axis=0)
        moved = None
        for piece in split3(block):
            part = lax.dot_general(
                order, piece, (((1,), (1,)), ((), ())), preferred_element_type=F32
            )
            moved = part if moved is None else moved + part
        state_ref[t] = moved * lane_scale(t, HALO)

    bias = jnp.concatenate([bias_ref[...]] * 8, axis=1)
    params = [far_ref[...], after_ref[HALO], before_ref[HALO]]
    second_ref[...] = jnp.zeros(second_ref.shape, BF16)

    def masked(value, pair, margin):
        halves = []
        scales = [row_scale(2 * pair + i - margin) for i in range(2)]
        if scales[0] is None and scales[1] is None:
            return value
        for i in range(2):
            half = value[:, 128 * i : 128 * (i + 1)]
            halves.append(half if scales[i] is None else half * scales[i])
        return jnp.concatenate(halves, axis=1)

    def keep_first(value, pair, margin):
        value = masked(half_silu(value), pair, margin)
        first_ref[pair, GRAIN : GRAIN + COLS, :] = value.astype(BF16)
        first_ref[pair, 0:GRAIN, :] = shifted_rows(value[COLS - GRAIN :], 1).astype(BF16)
        first_ref[pair, GRAIN + COLS :, :] = shifted_rows(value[:GRAIN], -1).astype(BF16)

    for step in range(ITERS):
        halo = HALO - 3 * step
        count = rows + 2 * halo
        tiles = pl.cdiv(count, 8)
        pairs = (count - 2) // 2
        active = jnp.where(time - ITERS + step >= 0, 1.0, 0.0)
        embed = params[step][0:1] * 0.5
        embed = jnp.concatenate([embed, embed], axis=1)
        keep = params[step][1:2] * active
        rate = params[step][2:3] * active

        for t in range(tiles):
            z = state_ref[t]
            zb_ref[t, GRAIN : GRAIN + COLS, :] = z.astype(BF16)
            zb_ref[t, 0:GRAIN, :] = shifted_rows(z[COLS - GRAIN :], 1).astype(BF16)
            zb_ref[t, GRAIN + COLS :, :] = shifted_rows(z[:GRAIN], -1).astype(BF16)

        def three(t):
            return jnp.concatenate(
                [zb_ref[t, GRAIN * b : GRAIN * b + COLS, :] for b in range(3)], axis=1
            )

        for t in range(tiles):
            here = min(3, pairs - 4 * t)
            if here > 0:
                out = jnp.dot(
                    three(t), w1a_ref[:, : 256 * here], preferred_element_type=F32
                )
                for i in range(here):
                    value = out[:, 256 * i : 256 * (i + 1)] + embed
                    keep_first(value, 4 * t + i, halo - 1)
            if 4 * t + 3 < pairs:
                both = jnp.concatenate([lane < 64] * 3, axis=1)
                out = jnp.dot(
                    jnp.where(both, three(t + 1), three(t)),
                    w1b_ref[...],
                    preferred_element_type=F32,
                )
                keep_first(out + embed, 4 * t + 3, halo - 1)

        chunk = (pairs - 1) // 3
        for start in range(0, pairs - 1, chunk):
            lhs = jnp.concatenate(
                [
                    jnp.concatenate(
                        [
                            first_ref[p + i, GRAIN * b : GRAIN * b + COLS, :]
                            for b in range(3)
                            for i in range(2)
                        ],
                        axis=1,
                    )
                    for p in range(start, start + chunk)
                ],
                axis=0,
            )
            out = jnp.dot(lhs, wm_ref[...], preferred_element_type=F32)
            for i in range(chunk):
                value = masked(
                    half_silu(out[COLS * i : COLS * (i + 1)]), start + i, halo - 2
                )
                second_ref[start + i] = value.astype(BF16)

        new_count = count - 6
        new_tiles = pl.cdiv(new_count, 8)
        lhs = jnp.concatenate(
            [
                jnp.concatenate([second_ref[4 * t + i] for i in range(5)], axis=1)
                for t in range(new_tiles)
            ],
            axis=0,
        )
        out = jnp.dot(lhs, w3_ref[...], preferred_element_type=F32)
        for t in range(new_tiles):
            g = out[COLS * t : COLS * (t + 1)]
            left = g[:, 0:128]
            right = g[:, 256:384]
            left = jnp.concatenate(
                [shifted_rows(left[COLS - GRAIN :], 1), left[: COLS - GRAIN]], axis=0
            )
            right = jnp.concatenate([right[GRAIN:], shifted_rows(right[:GRAIN], -1)], axis=0)
            conv = left + g[:, 128:256] + right
            here = state_ref[t]
            old = jnp.concatenate([here[:, 48:], state_ref[t + 1][:, :48]], axis=1) if (
                t + 1 < tiles
            ) else jnp.concatenate([here[:, 48:], jnp.zeros((COLS, 48), F32)], axis=1)
            new = old + keep * old + rate * (old + conv + bias)
            if step + 1 < ITERS:
                state_ref[t] = new * lane_scale(t, halo - 3)
            else:
                turned = new.T
                moved = None
                for piece in split3(turned):
                    part = jnp.dot(piece, order, preferred_element_type=F32)
                    moved = part if moved is None else moved + part
                for r in range(8):
                    out_ref[0, :, 8 * t + r, :] = moved[16 * r : 16 * r + 16]


def chain(
    start_noise, time_embed, keep_rate, denoise_rate, conv_first, conv_middle, conv_last, out_bias
):
    channels, rows, cols = start_noise.shape
    tm_size = lax.axis_size("tm")
    space_size = lax.axis_size("space")
    vmem = pl.BlockSpec(memory_space=pltpu.VMEM)
    smem = pl.BlockSpec(memory_space=pltpu.SMEM)
    shape = jax.ShapeDtypeStruct

    up, down, far = pl.pallas_call(
        pack_kernel,
        out_shape=(
            shape((HALO + 1, channels, cols), F32),
            shape((HALO + 1, channels, cols), F32),
            shape((8, cols), F32),
        ),
        in_specs=[vmem, vmem, smem, smem],
        out_specs=(vmem, vmem, vmem),
    )(start_noise, time_embed, keep_rate, denoise_rate)

    def moves(times, tiles):
        pairs = []
        for t in range(tm_size):
            for s in range(space_size):
                target = ((t + times) % tm_size) * space_size + (s + tiles) % space_size
                pairs.append((t * space_size + s, target))
        return pairs

    axes = ("tm", "space")
    before = lax.ppermute(up, axes, moves(1, 1))
    after = lax.ppermute(down, axes, moves(2, -1))
    far = lax.ppermute(far, axes, moves(3, 0))

    w1a, w1b, wm, w3 = pl.pallas_call(
        weights_kernel,
        out_shape=(
            shape((384, 768), BF16),
            shape((384, 256), BF16),
            shape((1536, 256), BF16),
            shape((1280, 384), BF16),
        ),
        in_specs=[vmem] * 3,
        out_specs=(vmem,) * 4,
    )(conv_first, conv_middle, conv_last)

    place = jnp.stack([lax.axis_index("tm"), lax.axis_index("space")]).astype(jnp.int32)
    total = rows + 2 * HALO
    pairs = (total - 2) // 2

    def body(*refs):
        chain_kernel(tm_size, space_size, rows, *refs)

    return pl.pallas_call(
        body,
        out_shape=shape((1, channels, rows, cols), F32),
        in_specs=[vmem] * 4 + [smem] + [vmem] * 5,
        out_specs=vmem,
        scratch_shapes=[
            pltpu.VMEM((pl.cdiv(total, 8), COLS, COLS), F32),
            pltpu.VMEM((pl.cdiv(total, 8), PAD, COLS), BF16),
            pltpu.VMEM((pairs, PAD, 256), BF16),
            pltpu.VMEM((pairs + 1, COLS, 256), BF16),
        ],
        compiler_params=pltpu.CompilerParams(vmem_limit_bytes=48 << 20),
    )(start_noise, before, after, far, place, out_bias.reshape(1, channels), w1a, w1b, wm, w3)


def solution(mesh):
    placed = (
        P(None, ("groups", "space"), None),
        P("tm", None),
        P("tm"),
        P("tm"),
        P(),
        P(),
        P(),
        P(),
    )
    return jax.shard_map(
        chain if mesh.shape["tm"] == ITERS + 1 else picard,
        mesh=mesh,
        in_specs=placed,
        out_specs=P("tm", None, ("groups", "space"), None),
        check_vma=False,
    )
```

time: 95.9 us -> 31.3 us (0.33)
  the two profiles are of different devices: /device:TPU:1 before, /device:TPU:0 now
where the time goes in v1:
time: 31.3 us; the launch traced here: 31 us
  Pallas kernels  15.5 us (50%)
  starting transfers between devices  7.58 us (24%)
  local copies, waits for them, and re-layouts  5.89 us (19%)
  between operations  1.32 us (4%)
  waiting for transfers between devices  0.64 us (2%)
    pallas_call x1, Pallas kernels, chain(): pl.pallas_call(body, out_shape=shape((1, channels, rows, cols), F32), in_...  11 us
    unnamed x17, local copies, waits for them, and re-layouts  5.89 us
    ppermute x1, starting transfers between devices, chain(): after = lax.ppermute(down, axes, moves(2, -1))  3.77 us
    pallas_call x1, Pallas kernels, chain(): pl.pallas_call(weights_kernel, out_shape=(shape((384, 768), BF16), shape(...  2.81 us
    ppermute x1, starting transfers between devices, chain(): before = lax.ppermute(up, axes, moves(1, 1))  2.46 us
    pallas_call x1, Pallas kernels, chain(): pl.pallas_call(pack_kernel, out_shape=(shape((HALO + 1, channels, cols),...  1.65 us
    ppermute x1, starting transfers between devices, chain(): far = lax.ppermute(far, axes, moves(3, 0))  1.35 us
    ppermute x1, waiting for transfers between devices, chain(): after = lax.ppermute(down, axes, moves(2, -1))  0.63 us
  transfers between devices with their start and end apart: 3, of which 1 were waited for; matrix products, arithmetic and copies ran while one was open for 3% of the time, Pallas kernels for 9%

profile of v1, /device:TPU:0, one launch (start us, length us, event | category | flops | bytes accessed | tf_op | source)
XLA Modules:
  0.0 31.0 jit_solution(15355654909306107070)
XLA Ops:
  1.3 0.0 copy-start.6
  1.3 1.6 %shard_map.82 = (f32[10,16,128]{2,1,0:T(8,128)}, f32[10,16,128]{2,1,0:T(8,128)}, f32[8,128]{1,0:T(8,128)}) custom-call(f32[16,16,128]{2,1,0:T(8,128)} %refs_0_.1, f32[1,128]{1,0:T(1,128)} %embed_ref.1, f32[1]{0:T(128)S(6)} %copy.10.keep_ref, f32[1]{0:T(128)S(6)} %copy.11.rate_ref), custom_call_target="tpu_custom_call" | custom-call | tf_op jit(solution)/shard_map/pallas_call | solution.py:344
  3.0 0.0 copy-start.7
  3.0 2.5 %collective-permute-start = (f32[10,16,128]{2,1,0:T(8,128)}, f32[10,16,128]{2,1,0:T(8,128)S(1)}, u32[]{:S(2)}, u32[]{:S(2)}) collective-permute-start(f32[10,16,128]{2,1,0:T(8,128)} %get-tuple-element.12), channel_id=1, source_target_pairs={{0,5},{1,6},{2,7},{3,4},{4,9},{5,10},{6,11},{7,8},{8,13},{9,14},{1... | collective-permute-start | bytes 245768 | tf_op jit(solution)/shard_map/ppermute | solution.py:364
  5.4 3.8 %collective-permute-start.1 = (f32[10,16,128]{2,1,0:T(8,128)}, f32[10,16,128]{2,1,0:T(8,128)S(1)}, u32[]{:S(2)}, u32[]{:S(2)}) collective-permute-start(f32[10,16,128]{2,1,0:T(8,128)} %get-tuple-element.13), channel_id=1, source_target_pairs={{0,11},{1,8},{2,9},{3,10},{4,15},{5,12},{6,13},{7,14},{8,3},{9,0},... | collective-permute-start | bytes 245768 | tf_op jit(solution)/shard_map/ppermute | solution.py:365
  9.2 0.0 copy-done.7
  9.2 1.3 %collective-permute-start.2 = (f32[8,128]{1,0:T(8,128)S(1)}, f32[8,128]{1,0:T(8,128)S(1)}, u32[]{:S(2)}, u32[]{:S(2)}) collective-permute-start(f32[8,128]{1,0:T(8,128)S(1)} %copy-done.7), channel_id=1, source_target_pairs={{0,12},{1,13},{2,14},{3,15},{4,0},{5,1},{6,2},{7,3},{8,4},{9,5},{1... | collective-permute-start | bytes 12296 | tf_op jit(solution)/shard_map/ppermute | solution.py:366
  10.5 0.1 pad_add_fusion.refs_4_
  10.6 0.0 copy-done.6
  10.6 0.9 %copy.9.first_ref = bf16[9,128,16]{2,1,0:T(8,128)(2,1)} copy(bf16[9,128,16]{1,2,0:T(8,128)(2,1)S(1)} %copy-done.6) | data formatting | bytes 73728 | tf_op args[4]
  11.5 0.0 copy-start.3
  11.5 2.8 %shard_map.83 = (bf16[384,768]{1,0:T(8,128)(2,1)}, bf16[384,256]{1,0:T(8,128)(2,1)}, bf16[1536,256]{1,0:T(8,128)(2,1)}, bf16[1280,384]{1,0:T(8,128)(2,1)}) custom-call(bf16[9,128,16]{2,1,0:T(8,128)(2,1)} %copy.9.first_ref, bf16[9,128,128]{2,1,0:T(8,128)(2,1)} %middle_ref.1, bf16[9,16,128]{2,1,0:T(8,128)(2,1)} %last_ref.1), custom_call_target="tpu_custom_call" | custom-call | tf_op jit(solution)/shard_map/pallas_call | solution.py:368
  14.3 0.0 collective-permute-done.2.refs_3_
  14.3 0.0 collective-permute-done.refs_1_
  14.3 0.6 %collective-permute-done.1.refs_2_ = f32[10,16,128]{2,1,0:T(8,128)S(1)} collective-permute-done((f32[10,16,128]{2,1,0:T(8,128)}, f32[10,16,128]{2,1,0:T(8,128)S(1)}, u32[]{:S(2)}, u32[]{:S(2)}) %collective-permute-start.1) | collective-permute-done | bytes 81952 | tf_op jit(solution)/shard_map/ppermute | solution.py:365
  15.0 0.0 copy-start.5
  15.0 0.0 copy-done.3
  15.0 0.7 %copy-done.5 = f32[16]{0:T(128)S(1)} copy-done((f32[16]{0:T(128)S(1)}, f32[16]{0:T(128)}, u32[]{:S(2)}) %copy-start.5) | copy-done | bytes 88
  15.6 0.0 copy-start
  15.6 1.2 %copy-done = bf16[1280,384]{1,0:T(8,128)(2,1)S(1)} copy-done((bf16[1280,384]{1,0:T(8,128)(2,1)S(1)}, bf16[1280,384]{1,0:T(8,128)(2,1)}, u32[]{:S(2)}) %copy-start) | copy-done | bytes 983064
  16.8 0.0 copy-start.1
  16.8 1.1 %copy-done.1 = bf16[1536,256]{1,0:T(8,128)(2,1)S(1)} copy-done((bf16[1536,256]{1,0:T(8,128)(2,1)S(1)}, bf16[1536,256]{1,0:T(8,128)(2,1)}, u32[]{:S(2)}) %copy-start.1) | copy-done | bytes 786456
  18.0 0.0 copy-start.2
  18.0 1.1 %copy-done.2 = bf16[384,768]{1,0:T(8,128)(2,1)S(1)} copy-done((bf16[384,768]{1,0:T(8,128)(2,1)S(1)}, bf16[384,768]{1,0:T(8,128)(2,1)}, u32[]{:S(2)}) %copy-start.2) | copy-done | bytes 589848
  19.0 0.0 copy-start.4
  19.0 0.9 %copy-done.4 = bf16[384,256]{1,0:T(8,128)(2,1)S(1)} copy-done((bf16[384,256]{1,0:T(8,128)(2,1)S(1)}, bf16[384,256]{1,0:T(8,128)(2,1)}, u32[]{:S(2)}) %copy-start.4) | copy-done | bytes 196632
  20.0 11.0 %shard_map.84 = f32[1,16,16,128]{3,2,1,0:T(8,128)} custom-call(f32[16,16,128]{2,1,0:T(8,128)S(1)} %copy-done.3, f32[10,16,128]{2,1,0:T(8,128)S(1)} %collective-permute-done.refs_1_, f32[10,16,128]{2,1,0:T(8,128)S(1)} %collective-permute-done.1.refs_2_, f32[8,128]{1,0:T(8,128)S(1)} %collective-permute-done.2.refs_3_, s32[2]{0:T(128)S(1)} %pad_add_fusion.refs_4_, ...), custom_call_target="tpu_custom_call" | custom-call | tf_op jit(solution)/shard_map/pallas_call | solution.py:387
Async XLA Ops:
  1.3 9.3 %copy-start.6 = (bf16[9,128,16]{1,2,0:T(8,128)(2,1)S(1)}, bf16[9,128,16]{1,2,0:T(8,128)(2,1)}, u32[]{:S(2)}) copy-start(bf16[9,128,16]{1,2,0:T(8,128)(2,1)} %param.12) | copy-start | bytes 110596
  3.0 6.2 %copy-start.7 = (f32[8,128]{1,0:T(8,128)S(1)}, f32[8,128]{1,0:T(8,128)}, u32[]{:S(2)}) copy-start(f32[8,128]{1,0:T(8,128)} %get-tuple-element.14) | copy-start | bytes 12292
  3.0 11.4 %collective-permute-start = (f32[10,16,128]{2,1,0:T(8,128)}, f32[10,16,128]{2,1,0:T(8,128)S(1)}, u32[]{:S(2)}, u32[]{:S(2)}) collective-permute-start(f32[10,16,128]{2,1,0:T(8,128)} %get-tuple-element.12), channel_id=1, source_target_pairs={{0,5},{1,6},{2,7},{3,4},{4,9},{5,10},{6,11},{7,8},{8,13},{9,14},{1... | collective-permute-start | bytes 245768 | tf_op jit(solution)/shard_map/ppermute | solution.py:364
  5.4 9.5 %collective-permute-start.1 = (f32[10,16,128]{2,1,0:T(8,128)}, f32[10,16,128]{2,1,0:T(8,128)S(1)}, u32[]{:S(2)}, u32[]{:S(2)}) collective-permute-start(f32[10,16,128]{2,1,0:T(8,128)} %get-tuple-element.13), channel_id=1, source_target_pairs={{0,11},{1,8},{2,9},{3,10},{4,15},{5,12},{6,13},{7,14},{8,3},{9,0},... | collective-permute-start | bytes 245768 | tf_op jit(solution)/shard_map/ppermute | solution.py:365
  9.2 5.1 %collective-permute-start.2 = (f32[8,128]{1,0:T(8,128)S(1)}, f32[8,128]{1,0:T(8,128)S(1)}, u32[]{:S(2)}, u32[]{:S(2)}) collective-permute-start(f32[8,128]{1,0:T(8,128)S(1)} %copy-done.7), channel_id=1, source_target_pairs={{0,12},{1,13},{2,14},{3,15},{4,0},{5,1},{6,2},{7,3},{8,4},{9,5},{1... | collective-permute-start | bytes 12296 | tf_op jit(solution)/shard_map/ppermute | solution.py:366
  11.5 3.5 %copy-start.3 = (f32[16,16,128]{2,1,0:T(8,128)S(1)}, f32[16,16,128]{2,1,0:T(8,128)}, u32[]{:S(2)}) copy-start(f32[16,16,128]{2,1,0:T(8,128)} %refs_0_.1) | copy-start | bytes 393220
  15.0 0.7 %copy-start.5 = (f32[16]{0:T(128)S(1)}, f32[16]{0:T(128)}, u32[]{:S(2)}) copy-start(f32[16]{0:T(128)} %param.15) | copy-start | bytes 196
  15.6 1.2 %copy-start = (bf16[1280,384]{1,0:T(8,128)(2,1)S(1)}, bf16[1280,384]{1,0:T(8,128)(2,1)}, u32[]{:S(2)}) copy-start(bf16[1280,384]{1,0:T(8,128)(2,1)} %get-tuple-element.18.refs_9_) | copy-start | bytes 2949124
  16.8 1.1 %copy-start.1 = (bf16[1536,256]{1,0:T(8,128)(2,1)S(1)}, bf16[1536,256]{1,0:T(8,128)(2,1)}, u32[]{:S(2)}) copy-start(bf16[1536,256]{1,0:T(8,128)(2,1)} %get-tuple-element.17.refs_8_) | copy-start | bytes 2359300
  18.0 1.1 %copy-start.2 = (bf16[384,768]{1,0:T(8,128)(2,1)S(1)}, bf16[384,768]{1,0:T(8,128)(2,1)}, u32[]{:S(2)}) copy-start(bf16[384,768]{1,0:T(8,128)(2,1)} %get-tuple-element.15.refs_6_) | copy-start | bytes 1769476
  19.0 0.9 %copy-start.4 = (bf16[384,256]{1,0:T(8,128)(2,1)S(1)}, bf16[384,256]{1,0:T(8,128)(2,1)}, u32[]{:S(2)}) copy-start(bf16[384,256]{1,0:T(8,128)(2,1)} %get-tuple-element.16.refs_7_) | copy-start | bytes 589828

commit v2 on v1

--- a/solution.py
+++ b/solution.py
@@ -98,12 +98,15 @@
     far_ref[...] = params
 
 
-def weights_kernel(first_ref, middle_ref, last_ref, w1a_ref, w1b_ref, wm_ref, w3_ref):
+def weights_kernel(
+    first_ref, middle_ref, last_ref, bias_in_ref, w1a_ref, w1b_ref, wm_ref, w3_ref, bias_ref
+):
+    bias_ref[...] = jnp.concatenate([bias_in_ref[...]] * 8, axis=1)
     w1a_ref[...] = jnp.zeros(w1a_ref.shape, BF16)
     w1b_ref[...] = jnp.zeros(w1b_ref.shape, BF16)
     for tap in range(9):
         a, b = divmod(tap, 3)
-        block = (first_ref[tap].astype(F32).T * 0.5).astype(BF16)
+        block = first_ref[tap] * BF16(0.5)
         for out in range(6):
             row = out + a
             w1a_ref[pl.ds(128 * b + 16 * row, 16), pl.ds(128 * out, 128)] = block
@@ -212,7 +215,7 @@
             moved = part if moved is None else moved + part
         state_ref[t] = moved * lane_scale(t, HALO)
 
-    bias = jnp.concatenate([bias_ref[...]] * 8, axis=1)
+    bias = bias_ref[...]
     params = [far_ref[...], after_ref[HALO], before_ref[HALO]]
     second_ref[...] = jnp.zeros(second_ref.shape, BF16)
 
@@ -344,9 +347,9 @@
     up, down, far = pl.pallas_call(
         pack_kernel,
         out_shape=(
-            shape((HALO + 1, channels, cols), F32),
-            shape((HALO + 1, channels, cols), F32),
-            shape((8, cols), F32),
+            pltpu.VMEM((HALO + 1, channels, cols), F32),
+            pltpu.VMEM((HALO + 1, channels, cols), F32),
+            pltpu.VMEM((8, cols), F32),
         ),
         in_specs=[vmem, vmem, smem, smem],
         out_specs=(vmem, vmem, vmem),
@@ -365,17 +368,18 @@
     after = lax.ppermute(down, axes, moves(2, -1))
     far = lax.ppermute(far, axes, moves(3, 0))
 
-    w1a, w1b, wm, w3 = pl.pallas_call(
+    w1a, w1b, wm, w3, bias = pl.pallas_call(
         weights_kernel,
         out_shape=(
-            shape((384, 768), BF16),
-            shape((384, 256), BF16),
-            shape((1536, 256), BF16),
-            shape((1280, 384), BF16),
+            pltpu.VMEM((384, 768), BF16),
+            pltpu.VMEM((384, 256), BF16),
+            pltpu.VMEM((1536, 256), BF16),
+            pltpu.VMEM((1280, 384), BF16),
+            pltpu.VMEM((1, COLS), F32),
         ),
-        in_specs=[vmem] * 3,
-        out_specs=(vmem,) * 4,
-    )(conv_first, conv_middle, conv_last)
+        in_specs=[vmem] * 4,
+        out_specs=(vmem,) * 5,
+    )(jnp.swapaxes(conv_first, 1, 2), conv_middle, conv_last, out_bias.reshape(1, channels))
 
     place = jnp.stack([lax.axis_index("tm"), lax.axis_index("space")]).astype(jnp.int32)
     total = rows + 2 * HALO
@@ -396,7 +400,7 @@
             pltpu.VMEM((pairs + 1, COLS, 256), BF16),
         ],
         compiler_params=pltpu.CompilerParams(vmem_limit_bytes=48 << 20),
-    )(start_noise, before, after, far, place, out_bias.reshape(1, channels), w1a, w1b, wm, w3)
+    )(start_noise, before, after, far, place, bias, w1a, w1b, wm, w3)
 
 
 def solution(mesh):

time: 31.3 us -> 27.5 us (0.88)
  the two profiles are of different devices: /device:TPU:0 before, /device:TPU:1 now
where the time goes in v2:
time: 27.5 us; the launch traced here: 27.3 us
  Pallas kernels  13.6 us (49%)
  waiting for transfers between devices  7.36 us (27%)
  starting transfers between devices  4.94 us (18%)
  between operations  1.32 us (5%)
    pallas_call x1, Pallas kernels, chain(): pl.pallas_call(body, out_shape=shape((1, channels, rows, cols), F32), in_...  11.1 us
    ppermute x1, starting transfers between devices, chain(): far = lax.ppermute(far, axes, moves(3, 0))  4.2 us
    ppermute x1, waiting for transfers between devices, chain(): after = lax.ppermute(down, axes, moves(2, -1))  4 us
    ppermute x1, waiting for transfers between devices, chain(): before = lax.ppermute(up, axes, moves(1, 1))  3.36 us
    pallas_call x1, Pallas kernels, chain(): pl.pallas_call(weights_kernel, out_shape=(pltpu.VMEM((384, 768), BF16), p...  1.57 us
    pallas_call x1, Pallas kernels, chain(): pl.pallas_call(pack_kernel, out_shape=(pltpu.VMEM((HALO + 1, channels, co...  0.99 us
    ppermute x1, starting transfers between devices, chain(): after = lax.ppermute(down, axes, moves(2, -1))  0.73 us
  transfers between devices with their start and end apart: 3, of which 2 were waited for; matrix products, arithmetic and copies ran while one was open for 0% of the time, Pallas kernels for 6%

profile of v2, /device:TPU:1, one launch (start us, length us, event | category | flops | bytes accessed | tf_op | source)
XLA Modules:
  0.0 27.3 jit_solution(5091874807800459811)
XLA Ops:
  1.3 1.0 %shard_map.82 = (f32[10,16,128]{2,1,0:T(8,128)S(1)}, f32[10,16,128]{2,1,0:T(8,128)S(1)}, f32[8,128]{1,0:T(8,128)S(1)}) custom-call(f32[16,16,128]{2,1,0:T(8,128)} %refs_0_.1, f32[1,128]{1,0:T(1,128)} %embed_ref.1, f32[1]{0:T(128)S(6)} %copy.9.keep_ref, f32[1]{0:T(128)S(6)} %copy.10.rate_ref), custom_call_target="tpu_custom_call" | custom-call | tf_op jit(solution)/shard_map/pallas_call | solution.py:347
  2.3 4.2 %collective-permute-start.2 = (f32[8,128]{1,0:T(8,128)S(1)}, f32[8,128]{1,0:T(8,128)S(1)}, u32[]{:S(2)}, u32[]{:S(2)}) collective-permute-start(f32[8,128]{1,0:T(8,128)S(1)} %get-tuple-element.15), channel_id=1, source_target_pairs={{0,12},{1,13},{2,14},{3,15},{4,0},{5,1},{6,2},{7,3},{8,4},{9,5},{1... | collective-permute-start | bytes 12296 | tf_op jit(solution)/shard_map/ppermute | solution.py:369
  6.5 0.0 collective-permute-start
  6.5 0.7 %collective-permute-start.1 = (f32[10,16,128]{2,1,0:T(8,128)S(1)}, f32[10,16,128]{2,1,0:T(8,128)S(1)}, u32[]{:S(2)}, u32[]{:S(2)}) collective-permute-start(f32[10,16,128]{2,1,0:T(8,128)S(1)} %get-tuple-element.14), channel_id=1, source_target_pairs={{0,11},{1,8},{2,9},{3,10},{4,15},{5,12},{6,13},{7,14},{8,3},{9,0},... | collective-permute-start | bytes 245768 | tf_op jit(solution)/shard_map/ppermute | solution.py:368
  7.2 0.1 pad_add_fusion.refs_4_
  7.3 0.0 copy-start
  7.3 1.6 %shard_map.83 = (bf16[384,768]{1,0:T(8,128)(2,1)S(1)}, bf16[384,256]{1,0:T(8,128)(2,1)S(1)}, bf16[1536,256]{1,0:T(8,128)(2,1)S(1)}, bf16[1280,384]{1,0:T(8,128)(2,1)S(1)}, f32[1,128]{1,0:T(1,128)S(1)}) custom-call(bf16[9,16,128]{2,1,0:T(8,128)(2,1)} %bitcast.4, bf16[9,128,128]{2,1,0:T(8,128)(2,1)} %middle_ref.1, bf16[9,16,128]{2,1,0:T(8,128)(2,1)} %last_ref.1, ...), custom_call_target="tpu_custom_call" | custom-call | tf_op jit(solution)/shard_map/pallas_call | solution.py:371
  8.9 0.0 collective-permute-done.2.refs_3_
  8.9 3.4 %collective-permute-done.refs_1_ = f32[10,16,128]{2,1,0:T(8,128)S(1)} collective-permute-done((f32[10,16,128]{2,1,0:T(8,128)S(1)}, f32[10,16,128]{2,1,0:T(8,128)S(1)}, u32[]{:S(2)}, u32[]{:S(2)}) %collective-permute-start) | collective-permute-done | bytes 81952 | tf_op jit(solution)/shard_map/ppermute | solution.py:367
  12.3 4.0 %collective-permute-done.1.refs_2_ = f32[10,16,128]{2,1,0:T(8,128)S(1)} collective-permute-done((f32[10,16,128]{2,1,0:T(8,128)S(1)}, f32[10,16,128]{2,1,0:T(8,128)S(1)}, u32[]{:S(2)}, u32[]{:S(2)}) %collective-permute-start.1) | collective-permute-done | bytes 81952 | tf_op jit(solution)/shard_map/ppermute | solution.py:368
  16.3 0.0 copy-done
  16.3 11.1 %shard_map.84 = f32[1,16,16,128]{3,2,1,0:T(8,128)} custom-call(f32[16,16,128]{2,1,0:T(8,128)S(1)} %copy-done, f32[10,16,128]{2,1,0:T(8,128)S(1)} %collective-permute-done.refs_1_, f32[10,16,128]{2,1,0:T(8,128)S(1)} %collective-permute-done.1.refs_2_, f32[8,128]{1,0:T(8,128)S(1)} %collective-permute-done.2.refs_3_, s32[2]{0:T(128)S(1)} %pad_add_fusion.refs_4_, ...), custom_call_target="tpu_custom_call" | custom-call | tf_op jit(solution)/shard_map/pallas_call | solution.py:391
Async XLA Ops:
  2.3 6.6 %collective-permute-start.2 = (f32[8,128]{1,0:T(8,128)S(1)}, f32[8,128]{1,0:T(8,128)S(1)}, u32[]{:S(2)}, u32[]{:S(2)}) collective-permute-start(f32[8,128]{1,0:T(8,128)S(1)} %get-tuple-element.15), channel_id=1, source_target_pairs={{0,12},{1,13},{2,14},{3,15},{4,0},{5,1},{6,2},{7,3},{8,4},{9,5},{1... | collective-permute-start | bytes 12296 | tf_op jit(solution)/shard_map/ppermute | solution.py:369
  6.5 5.8 %collective-permute-start = (f32[10,16,128]{2,1,0:T(8,128)S(1)}, f32[10,16,128]{2,1,0:T(8,128)S(1)}, u32[]{:S(2)}, u32[]{:S(2)}) collective-permute-start(f32[10,16,128]{2,1,0:T(8,128)S(1)} %get-tuple-element.13), channel_id=1, source_target_pairs={{0,5},{1,6},{2,7},{3,4},{4,9},{5,10},{6,11},{7,8},{8,13},{9,14},{1... | collective-permute-start | bytes 245768 | tf_op jit(solution)/shard_map/ppermute | solution.py:367
  6.5 9.8 %collective-permute-start.1 = (f32[10,16,128]{2,1,0:T(8,128)S(1)}, f32[10,16,128]{2,1,0:T(8,128)S(1)}, u32[]{:S(2)}, u32[]{:S(2)}) collective-permute-start(f32[10,16,128]{2,1,0:T(8,128)S(1)} %get-tuple-element.14), channel_id=1, source_target_pairs={{0,11},{1,8},{2,9},{3,10},{4,15},{5,12},{6,13},{7,14},{8,3},{9,0},... | collective-permute-start | bytes 245768 | tf_op jit(solution)/shard_map/ppermute | solution.py:368
  7.3 9.0 %copy-start = (f32[16,16,128]{2,1,0:T(8,128)S(1)}, f32[16,16,128]{2,1,0:T(8,128)}, u32[]{:S(2)}) copy-start(f32[16,16,128]{2,1,0:T(8,128)} %refs_0_.1) | copy-start | bytes 393220

commit v3 on v2

--- a/solution.py
+++ b/solution.py
@@ -194,30 +194,30 @@
         rel = lane_row + (8 * tile_index - halo)
         return jnp.where(rel < 0, top, jnp.where(rel >= rows, bottom, 1.0))
 
-    total = rows + 2 * HALO
-    for t in range(pl.cdiv(total, 8)):
-        parts = []
-        for e in range(8 * t, 8 * t + 8):
-            if e < HALO:
-                parts.append(before_ref[e])
-            elif e < HALO + rows:
-                parts.append(noise_ref[:, e - HALO, :])
-            elif e < total:
-                parts.append(after_ref[e - HALO - rows])
-            else:
-                parts.append(jnp.zeros((16, COLS), F32))
-        block = jnp.concatenate(parts, axis=0)
-        moved = None
-        for piece in split3(block):
-            part = lax.dot_general(
-                order, piece, (((1,), (1,)), ((), ())), preferred_element_type=F32
-            )
-            moved = part if moved is None else moved + part
-        state_ref[t] = moved * lane_scale(t, HALO)
+    def build_state(halo):
+        total = rows + 2 * halo
+        for t in range(pl.cdiv(total, 8)):
+            parts = []
+            for e in range(8 * t, 8 * t + 8):
+                if e < halo:
+                    parts.append(before_ref[HALO - halo + e])
+                elif e < halo + rows:
+                    parts.append(noise_ref[:, e - halo, :])
+                elif e < total:
+                    parts.append(after_ref[e - halo - rows])
+                else:
+                    parts.append(jnp.zeros((16, COLS), F32))
+            block = jnp.concatenate(parts, axis=0)
+            moved = None
+            for piece in split3(block):
+                part = lax.dot_general(
+                    order, piece, (((1,), (1,)), ((), ())), preferred_element_type=F32
+                )
+                moved = part if moved is None else moved + part
+            state_ref[t] = moved * lane_scale(t, halo)
 
     bias = bias_ref[...]
     params = [far_ref[...], after_ref[HALO], before_ref[HALO]]
-    second_ref[...] = jnp.zeros(second_ref.shape, BF16)
 
     def masked(value, pair, margin):
         halves = []
@@ -235,16 +235,15 @@
         first_ref[pair, 0:GRAIN, :] = shifted_rows(value[COLS - GRAIN :], 1).astype(BF16)
         first_ref[pair, GRAIN + COLS :, :] = shifted_rows(value[:GRAIN], -1).astype(BF16)
 
-    for step in range(ITERS):
+    def one_step(step):
         halo = HALO - 3 * step
         count = rows + 2 * halo
         tiles = pl.cdiv(count, 8)
         pairs = (count - 2) // 2
-        active = jnp.where(time - ITERS + step >= 0, 1.0, 0.0)
         embed = params[step][0:1] * 0.5
         embed = jnp.concatenate([embed, embed], axis=1)
-        keep = params[step][1:2] * active
-        rate = params[step][2:3] * active
+        keep = params[step][1:2]
+        rate = params[step][2:3]
 
         for t in range(tiles):
             z = state_ref[t]
@@ -300,6 +299,8 @@
 
         new_count = count - 6
         new_tiles = pl.cdiv(new_count, 8)
+        for i in range(pairs - 1, 4 * new_tiles + 1):
+            second_ref[i] = jnp.zeros((COLS, 256), BF16)
         lhs = jnp.concatenate(
             [
                 jnp.concatenate([second_ref[4 * t + i] for i in range(5)], axis=1)
@@ -333,6 +334,20 @@
                 for r in range(8):
                     out_ref[0, :, 8 * t + r, :] = moved[16 * r : 16 * r + 16]
 
+    for step in range(ITERS):
+
+        @pl.when(time == ITERS - step)
+        def _():
+            build_state(HALO - 3 * step)
+
+        @pl.when(time >= ITERS - step)
+        def _():
+            one_step(step)
+
+    @pl.when(time == 0)
+    def _():
+        out_ref[0] = noise_ref[...]
+
 
 def chain(
     start_noise, time_embed, keep_rate, denoise_rate, conv_first, conv_middle, conv_last, out_bias
@@ -356,17 +371,16 @@
     )(start_noise, time_embed, keep_rate, denoise_rate)
 
     def moves(times, tiles):
-        pairs = []
-        for t in range(tm_size):
-            for s in range(space_size):
-                target = ((t + times) % tm_size) * space_size + (s + tiles) % space_size
-                pairs.append((t * space_size + s, target))
-        return pairs
+        return [
+            (t * space_size + s, u * space_size + (s + tiles) % space_size)
+            for t, u in times
+            for s in range(space_size)
+        ]
 
     axes = ("tm", "space")
-    before = lax.ppermute(up, axes, moves(1, 1))
-    after = lax.ppermute(down, axes, moves(2, -1))
-    far = lax.ppermute(far, axes, moves(3, 0))
+    before = lax.ppermute(up, axes, moves([(0, 1), (1, 2), (2, 3)], 1))
+    after = lax.ppermute(down, axes, moves([(0, 2), (1, 3), (2, 1)], -1))
+    far = lax.ppermute(far, axes, moves([(0, 3)], 0))
 
     w1a, w1b, wm, w3, bias = pl.pallas_call(
         weights_kernel,

time: 27.5 us -> 26.1 us (0.949)
  the two profiles are of different devices: /device:TPU:1 before, /device:TPU:25 now
where the time goes in v3:
time: 26.1 us; the launch traced here: 25.9 us
  Pallas kernels  14.3 us (55%)
  waiting for transfers between devices  6.33 us (24%)
  starting transfers between devices  3.88 us (15%)
  between operations  1.34 us (5%)
    pallas_call x1, Pallas kernels, chain(): pl.pallas_call(body, out_shape=shape((1, channels, rows, cols), F32), in_...  11.7 us
    ppermute x1, waiting for transfers between devices, chain(): after = lax.ppermute(down, axes, moves([(0, 2), (1, 3), (2, 1)], -1))  4.51 us
    pallas_call x1, Pallas kernels, chain(): pl.pallas_call(weights_kernel, out_shape=(pltpu.VMEM((384, 768), BF16), p...  1.57 us
    ppermute x1, starting transfers between devices, chain(): far = lax.ppermute(far, axes, moves([(0, 3)], 0))  1.29 us
    ppermute x1, starting transfers between devices, chain(): before = lax.ppermute(up, axes, moves([(0, 1), (1, 2), (2, 3)], 1))  1.29 us
    ppermute x1, starting transfers between devices, chain(): after = lax.ppermute(down, axes, moves([(0, 2), (1, 3), (2, 1)], -1))  1.29 us
    ppermute x1, waiting for transfers between devices, chain(): before = lax.ppermute(up, axes, moves([(0, 1), (1, 2), (2, 3)], 1))  1.03 us
    pallas_call x1, Pallas kernels, chain(): pl.pallas_call(pack_kernel, out_shape=(pltpu.VMEM((HALO + 1, channels, co...  0.99 us
  transfers between devices with their start and end apart: 3, of which 3 were waited for; matrix products, arithmetic and copies ran while one was open for 0% of the time, Pallas kernels for 6%

profile of v3, /device:TPU:25, one launch (start us, length us, event | category | flops | bytes accessed | tf_op | source)
XLA Modules:
  0.0 25.9 jit_solution(9647252488774703580)
XLA Ops:
  1.3 1.0 %shard_map.82 = (f32[10,16,128]{2,1,0:T(8,128)S(1)}, f32[10,16,128]{2,1,0:T(8,128)S(1)}, f32[8,128]{1,0:T(8,128)S(1)}) custom-call(f32[16,16,128]{2,1,0:T(8,128)} %refs_0_.1, f32[1,128]{1,0:T(1,128)} %embed_ref.1, f32[1]{0:T(128)S(6)} %copy.9.keep_ref, f32[1]{0:T(128)S(6)} %copy.10.rate_ref), custom_call_target="tpu_custom_call" | custom-call | tf_op jit(solution)/shard_map/pallas_call | solution.py:362
  2.3 1.3 %collective-permute-start.2 = (f32[8,128]{1,0:T(8,128)S(1)}, f32[8,128]{1,0:T(8,128)S(1)}, u32[]{:S(2)}, u32[]{:S(2)}) collective-permute-start(f32[8,128]{1,0:T(8,128)S(1)} %get-tuple-element.15), channel_id=1, source_target_pairs={{0,12},{1,13},{2,14},{3,15},{16,28},{17,29},{18,30},{19,31}} | collective-permute-start | bytes 12296 | tf_op jit(solution)/shard_map/ppermute | solution.py:383
  3.6 1.3 %collective-permute-start = (f32[10,16,128]{2,1,0:T(8,128)S(1)}, f32[10,16,128]{2,1,0:T(8,128)S(1)}, u32[]{:S(2)}, u32[]{:S(2)}) collective-permute-start(f32[10,16,128]{2,1,0:T(8,128)S(1)} %get-tuple-element.13), channel_id=1, source_target_pairs={{0,5},{1,6},{2,7},{3,4},{4,9},{5,10},{6,11},{7,8},{8,13},{9,14},{1... | collective-permute-start | bytes 245768 | tf_op jit(solution)/shard_map/ppermute | solution.py:381
  4.9 1.3 %collective-permute-start.1 = (f32[10,16,128]{2,1,0:T(8,128)S(1)}, f32[10,16,128]{2,1,0:T(8,128)S(1)}, u32[]{:S(2)}, u32[]{:S(2)}) collective-permute-start(f32[10,16,128]{2,1,0:T(8,128)S(1)} %get-tuple-element.14), channel_id=1, source_target_pairs={{0,11},{1,8},{2,9},{3,10},{4,15},{5,12},{6,13},{7,14},{8,7},{9,4},... | collective-permute-start | bytes 245768 | tf_op jit(solution)/shard_map/ppermute | solution.py:382
  6.2 0.1 pad_add_fusion.refs_4_
  6.3 0.0 copy-start
  6.3 1.6 %shard_map.83 = (bf16[384,768]{1,0:T(8,128)(2,1)S(1)}, bf16[384,256]{1,0:T(8,128)(2,1)S(1)}, bf16[1536,256]{1,0:T(8,128)(2,1)S(1)}, bf16[1280,384]{1,0:T(8,128)(2,1)S(1)}, f32[1,128]{1,0:T(1,128)S(1)}) custom-call(bf16[9,16,128]{2,1,0:T(8,128)(2,1)} %bitcast.4, bf16[9,128,128]{2,1,0:T(8,128)(2,1)} %middle_ref.1, bf16[9,16,128]{2,1,0:T(8,128)(2,1)} %last_ref.1, ...), custom_call_target="tpu_custom_call" | custom-call | tf_op jit(solution)/shard_map/pallas_call | solution.py:385
  7.9 0.8 %collective-permute-done.2.refs_3_ = f32[8,128]{1,0:T(8,128)S(1)} collective-permute-done((f32[8,128]{1,0:T(8,128)S(1)}, f32[8,128]{1,0:T(8,128)S(1)}, u32[]{:S(2)}, u32[]{:S(2)}) %collective-permute-start.2) | collective-permute-done | bytes 4128 | tf_op jit(solution)/shard_map/ppermute | solution.py:383
  8.6 1.0 %collective-permute-done.refs_1_ = f32[10,16,128]{2,1,0:T(8,128)S(1)} collective-permute-done((f32[10,16,128]{2,1,0:T(8,128)S(1)}, f32[10,16,128]{2,1,0:T(8,128)S(1)}, u32[]{:S(2)}, u32[]{:S(2)}) %collective-permute-start) | collective-permute-done | bytes 81952 | tf_op jit(solution)/shard_map/ppermute | solution.py:381
  9.7 4.5 %collective-permute-done.1.refs_2_ = f32[10,16,128]{2,1,0:T(8,128)S(1)} collective-permute-done((f32[10,16,128]{2,1,0:T(8,128)S(1)}, f32[10,16,128]{2,1,0:T(8,128)S(1)}, u32[]{:S(2)}, u32[]{:S(2)}) %collective-permute-start.1) | collective-permute-done | bytes 81952 | tf_op jit(solution)/shard_map/ppermute | solution.py:382
  14.2 0.0 copy-done
  14.2 11.7 %shard_map.84 = f32[1,16,16,128]{3,2,1,0:T(8,128)} custom-call(f32[16,16,128]{2,1,0:T(8,128)S(1)} %copy-done, f32[10,16,128]{2,1,0:T(8,128)S(1)} %collective-permute-done.refs_1_, f32[10,16,128]{2,1,0:T(8,128)S(1)} %collective-permute-done.1.refs_2_, f32[8,128]{1,0:T(8,128)S(1)} %collective-permute-done.2.refs_3_, s32[2]{0:T(128)S(1)} %pad_add_fusion.refs_4_, ...), custom_call_target="tpu_custom_call" | custom-call | tf_op jit(solution)/shard_map/pallas_call | solution.py:405
Async XLA Ops:
  2.3 6.4 %collective-permute-start.2 = (f32[8,128]{1,0:T(8,128)S(1)}, f32[8,128]{1,0:T(8,128)S(1)}, u32[]{:S(2)}, u32[]{:S(2)}) collective-permute-start(f32[8,128]{1,0:T(8,128)S(1)} %get-tuple-element.15), channel_id=1, source_target_pairs={{0,12},{1,13},{2,14},{3,15},{16,28},{17,29},{18,30},{19,31}} | collective-permute-start | bytes 12296 | tf_op jit(solution)/shard_map/ppermute | solution.py:383
  3.6 6.1 %collective-permute-start = (f32[10,16,128]{2,1,0:T(8,128)S(1)}, f32[10,16,128]{2,1,0:T(8,128)S(1)}, u32[]{:S(2)}, u32[]{:S(2)}) collective-permute-start(f32[10,16,128]{2,1,0:T(8,128)S(1)} %get-tuple-element.13), channel_id=1, source_target_pairs={{0,5},{1,6},{2,7},{3,4},{4,9},{5,10},{6,11},{7,8},{8,13},{9,14},{1... | collective-permute-start | bytes 245768 | tf_op jit(solution)/shard_map/ppermute | solution.py:381
  4.9 9.3 %collective-permute-start.1 = (f32[10,16,128]{2,1,0:T(8,128)S(1)}, f32[10,16,128]{2,1,0:T(8,128)S(1)}, u32[]{:S(2)}, u32[]{:S(2)}) collective-permute-start(f32[10,16,128]{2,1,0:T(8,128)S(1)} %get-tuple-element.14), channel_id=1, source_target_pairs={{0,11},{1,8},{2,9},{3,10},{4,15},{5,12},{6,13},{7,14},{8,7},{9,4},... | collective-permute-start | bytes 245768 | tf_op jit(solution)/shard_map/ppermute | solution.py:382
  6.3 7.9 %copy-start = (f32[16,16,128]{2,1,0:T(8,128)S(1)}, f32[16,16,128]{2,1,0:T(8,128)}, u32[]{:S(2)}) copy-start(f32[16,16,128]{2,1,0:T(8,128)} %refs_0_.1) | copy-start | bytes 393220

commit v4 on v3

--- a/solution.py
+++ b/solution.py
@@ -76,26 +76,6 @@
 COLS = 128
 GRAIN = 16
 PAD = COLS + 2 * GRAIN
-
-
-def pack_kernel(noise_ref, embed_ref, keep_ref, rate_ref, up_ref, down_ref, far_ref):
-    rows = noise_ref.shape[1]
-    params = jnp.concatenate(
-        [
-            embed_ref[...],
-            jnp.full((1, COLS), keep_ref[0], F32),
-            jnp.full((1, COLS), rate_ref[0], F32),
-            jnp.zeros((5, COLS), F32),
-        ],
-        axis=0,
-    )
-    full = jnp.concatenate([params, jnp.zeros((8, COLS), F32)], axis=0)
-    for i in range(HALO):
-        up_ref[i] = noise_ref[:, rows - HALO + i, :]
-        down_ref[i] = noise_ref[:, i, :]
-    up_ref[HALO] = full
-    down_ref[HALO] = full
-    far_ref[...] = params
 
 
 def weights_kernel(
@@ -159,7 +139,9 @@
     noise_ref,
     before_ref,
     after_ref,
-    far_ref,
+    one_ref,
+    two_ref,
+    three_ref,
     place_ref,
     bias_ref,
     w1a_ref,
@@ -200,11 +182,11 @@
             parts = []
             for e in range(8 * t, 8 * t + 8):
                 if e < halo:
-                    parts.append(before_ref[HALO - halo + e])
+                    parts.append(before_ref[:, rows - halo + e, :])
                 elif e < halo + rows:
                     parts.append(noise_ref[:, e - halo, :])
                 elif e < total:
-                    parts.append(after_ref[e - halo - rows])
+                    parts.append(after_ref[:, e - halo - rows, :])
                 else:
                     parts.append(jnp.zeros((16, COLS), F32))
             block = jnp.concatenate(parts, axis=0)
@@ -217,7 +199,7 @@
             state_ref[t] = moved * lane_scale(t, halo)
 
     bias = bias_ref[...]
-    params = [far_ref[...], after_ref[HALO], before_ref[HALO]]
+    params = [two_ref[3:6], two_ref[0:3], one_ref[...]]
 
     def masked(value, pair, margin):
         halves = []
@@ -359,16 +341,14 @@
     smem = pl.BlockSpec(memory_space=pltpu.SMEM)
     shape = jax.ShapeDtypeStruct
 
-    up, down, far = pl.pallas_call(
-        pack_kernel,
-        out_shape=(
-            pltpu.VMEM((HALO + 1, channels, cols), F32),
-            pltpu.VMEM((HALO + 1, channels, cols), F32),
-            pltpu.VMEM((8, cols), F32),
-        ),
-        in_specs=[vmem, vmem, smem, smem],
-        out_specs=(vmem, vmem, vmem),
-    )(start_noise, time_embed, keep_rate, denoise_rate)
+    far = jnp.concatenate(
+        [
+            time_embed,
+            jnp.broadcast_to(keep_rate[:, None], (1, cols)),
+            jnp.broadcast_to(denoise_rate[:, None], (1, cols)),
+        ],
+        axis=0,
+    )
 
     def moves(times, tiles):
         return [
@@ -378,9 +358,13 @@
         ]
 
     axes = ("tm", "space")
-    before = lax.ppermute(up, axes, moves([(0, 1), (1, 2), (2, 3)], 1))
-    after = lax.ppermute(down, axes, moves([(0, 2), (1, 3), (2, 1)], -1))
-    far = lax.ppermute(far, axes, moves([(0, 3)], 0))
+    own = [(t, t) for t in range(tm_size)]
+    before = lax.ppermute(start_noise, axes, moves(own, 1))
+    after = lax.ppermute(start_noise, axes, moves(own, -1))
+    one = lax.ppermute(far, "tm", [(0, 1), (1, 2), (2, 3), (3, 0)])
+    both = jnp.concatenate([far, one], axis=0)
+    two = lax.ppermute(both, "tm", [(0, 2), (1, 3), (2, 0), (3, 1)])
+    three = one
 
     w1a, w1b, wm, w3, bias = pl.pallas_call(
         weights_kernel,
@@ -405,7 +389,7 @@
     return pl.pallas_call(
         body,
         out_shape=shape((1, channels, rows, cols), F32),
-        in_specs=[vmem] * 4 + [smem] + [vmem] * 5,
+        in_specs=[vmem] * 6 + [smem] + [vmem] * 5,
         out_specs=vmem,
         scratch_shapes=[
             pltpu.VMEM((pl.cdiv(total, 8), COLS, COLS), F32),
@@ -414,7 +398,7 @@
             pltpu.VMEM((pairs + 1, COLS, 256), BF16),
         ],
         compiler_params=pltpu.CompilerParams(vmem_limit_bytes=48 << 20),
-    )(start_noise, before, after, far, place, bias, w1a, w1b, wm, w3)
+    )(start_noise, before, after, one, two, three, place, bias, w1a, w1b, wm, w3)
 
 
 def solution(mesh):

time: 26.1 us -> 22.1 us (0.85)
  the two profiles are of different devices: /device:TPU:25 before, /device:TPU:24 now
where the time goes in v4:
time: 22.1 us; the launch traced here: 22 us
  Pallas kernels  13.3 us (60%)
  waiting for transfers between devices  4.29 us (19%)
  starting transfers between devices  2.24 us (10%)
  between operations  1.35 us (6%)
  local copies, waits for them, and re-layouts  0.65 us (3%)
    pallas_call x1, Pallas kernels, chain(): pl.pallas_call(body, out_shape=shape((1, channels, rows, cols), F32), in_...  11.8 us
    ppermute x1, waiting for transfers between devices, chain(): two = lax.ppermute(both, 'tm', [(0, 2), (1, 3), (2, 0), (3, 1)])  2.51 us
    ppermute x1, waiting for transfers between devices, chain(): one = lax.ppermute(far, 'tm', [(0, 1), (1, 2), (2, 3), (3, 0)])  1.77 us
    ppermute x1, starting transfers between devices, chain(): after = lax.ppermute(start_noise, axes, moves(own, -1))  1.73 us
    pallas_call x1, Pallas kernels, chain(): pl.pallas_call(weights_kernel, out_shape=(pltpu.VMEM((384, 768), BF16), p...  1.57 us
    unnamed x4, local copies, waits for them, and re-layouts  0.64 us
  transfers between devices with their start and end apart: 4, of which 2 were waited for; matrix products, arithmetic and copies ran while one was open for 0% of the time, Pallas kernels for 7%

profile of v4, /device:TPU:24, one launch (start us, length us, event | category | flops | bytes accessed | tf_op | source)
XLA Modules:
  0.0 22.0 jit_solution(3861940839630270711)
XLA Ops:
  1.3 0.0 copy-start.1
  1.3 0.6 %copy-done.1 = f32[1,128]{1,0:T(1,128)S(1)} copy-done((f32[1,128]{1,0:T(1,128)S(1)}, f32[1,128]{1,0:T(1,128)}, u32[]{:S(2)}) %copy-start.1) | copy-done | bytes 536
  2.0 0.1 collective-permute-start.2
  2.0 0.1 collective-permute-start
  2.1 1.7 %collective-permute-start.1 = (f32[16,16,128]{2,1,0:T(8,128)}, f32[16,16,128]{2,1,0:T(8,128)S(1)}, u32[]{:S(2)}, u32[]{:S(2)}) collective-permute-start(f32[16,16,128]{2,1,0:T(8,128)} %refs_0_.1), channel_id=1, source_target_pairs={{0,3},{1,0},{2,1},{3,2},{4,7},{5,4},{6,5},{7,6},{8,11},{9,8},{10,9... | collective-permute-start | bytes 393224 | tf_op jit(solution)/shard_map/ppermute | solution.py:363
  3.8 1.8 %collective-permute-done.2.refs_3_.refs_5_ = f32[3,128]{1,0:T(4,128)S(1)} collective-permute-done((f32[3,128]{1,0:T(4,128)S(1)}, f32[3,128]{1,0:T(4,128)S(1)}, u32[]{:S(2)}, u32[]{:S(2)}) %collective-permute-start.2) | collective-permute-done | bytes 1568 | tf_op jit(solution)/shard_map/ppermute | solution.py:364
  5.6 0.4 %collective-permute-start.3 = (f32[6,128]{1,0:T(8,128)S(1)}, f32[6,128]{1,0:T(8,128)S(1)}, u32[]{:S(2)}, u32[]{:S(2)}) collective-permute-start(f32[6,128]{1,0:T(8,128)S(1)} %pad_maximum_fusion), channel_id=1, source_target_pairs={{0,8},{4,12},{8,0},{12,4},{1,9},{5,13},{9,1},{13,5},{2,10},{6,14},... | collective-permute-start | bytes 9224 | tf_op jit(solution)/shard_map/ppermute | solution.py:366
  6.0 0.1 pad_add_fusion.refs_6_
  6.1 0.0 copy-start
  6.1 1.6 %shard_map.82 = (bf16[384,768]{1,0:T(8,128)(2,1)S(1)}, bf16[384,256]{1,0:T(8,128)(2,1)S(1)}, bf16[1536,256]{1,0:T(8,128)(2,1)S(1)}, bf16[1280,384]{1,0:T(8,128)(2,1)S(1)}, f32[1,128]{1,0:T(1,128)S(1)}) custom-call(bf16[9,16,128]{2,1,0:T(8,128)(2,1)} %bitcast.8, bf16[9,128,128]{2,1,0:T(8,128)(2,1)} %middle_ref.1, bf16[9,16,128]{2,1,0:T(8,128)(2,1)} %last_ref.1, ...), custom_call_target="tpu_custom_call" | custom-call | tf_op jit(solution)/shard_map/pallas_call | solution.py:369
  7.7 2.5 %collective-permute-done.3.refs_4_ = f32[6,128]{1,0:T(8,128)S(1)} collective-permute-done((f32[6,128]{1,0:T(8,128)S(1)}, f32[6,128]{1,0:T(8,128)S(1)}, u32[]{:S(2)}, u32[]{:S(2)}) %collective-permute-start.3) | collective-permute-done | bytes 3104 | tf_op jit(solution)/shard_map/ppermute | solution.py:366
  10.2 0.0 collective-permute-done.refs_1_
  10.2 0.0 collective-permute-done.1.refs_2_
  10.2 0.0 copy-done
  10.2 11.8 %shard_map.83 = f32[1,16,16,128]{3,2,1,0:T(8,128)} custom-call(f32[16,16,128]{2,1,0:T(8,128)S(1)} %copy-done, f32[16,16,128]{2,1,0:T(8,128)S(1)} %collective-permute-done.refs_1_, f32[16,16,128]{2,1,0:T(8,128)S(1)} %collective-permute-done.1.refs_2_, f32[3,128]{1,0:T(4,128)S(1)} %collective-permute-done.2.refs_3_.refs_5_, ...), custom_call_target="tpu_custom_call" | custom-call | tf_op jit(solution)/shard_map/pallas_call | solution.py:389
  (4 shorter events, 0.0 us)
Async XLA Ops:
  1.3 0.7 %copy-start.1 = (f32[1,128]{1,0:T(1,128)S(1)}, f32[1,128]{1,0:T(1,128)}, u32[]{:S(2)}) copy-start(f32[1,128]{1,0:T(1,128)} %param.9) | copy-start | bytes 1540
  2.0 3.6 %collective-permute-start.2 = (f32[3,128]{1,0:T(4,128)S(1)}, f32[3,128]{1,0:T(4,128)S(1)}, u32[]{:S(2)}, u32[]{:S(2)}) collective-permute-start(f32[3,128]{1,0:T(4,128)S(1)} %pad_maximum_fusion.1), channel_id=1, source_target_pairs={{0,4},{4,8},{8,12},{12,0},{1,5},{5,9},{9,13},{13,1},{2,6},{6,10},{... | collective-permute-start | bytes 4616 | tf_op jit(solution)/shard_map/ppermute | solution.py:364
  2.0 8.2 %collective-permute-start = (f32[16,16,128]{2,1,0:T(8,128)}, f32[16,16,128]{2,1,0:T(8,128)S(1)}, u32[]{:S(2)}, u32[]{:S(2)}) collective-permute-start(f32[16,16,128]{2,1,0:T(8,128)} %refs_0_.1), channel_id=1, source_target_pairs={{0,1},{1,2},{2,3},{3,0},{4,5},{5,6},{6,7},{7,4},{8,9},{9,10},{10,1... | collective-permute-start | bytes 393224 | tf_op jit(solution)/shard_map/ppermute | solution.py:362
  2.1 8.1 %collective-permute-start.1 = (f32[16,16,128]{2,1,0:T(8,128)}, f32[16,16,128]{2,1,0:T(8,128)S(1)}, u32[]{:S(2)}, u32[]{:S(2)}) collective-permute-start(f32[16,16,128]{2,1,0:T(8,128)} %refs_0_.1), channel_id=1, source_target_pairs={{0,3},{1,0},{2,1},{3,2},{4,7},{5,4},{6,5},{7,6},{8,11},{9,8},{10,9... | collective-permute-start | bytes 393224 | tf_op jit(solution)/shard_map/ppermute | solution.py:363
  5.6 4.6 %collective-permute-start.3 = (f32[6,128]{1,0:T(8,128)S(1)}, f32[6,128]{1,0:T(8,128)S(1)}, u32[]{:S(2)}, u32[]{:S(2)}) collective-permute-start(f32[6,128]{1,0:T(8,128)S(1)} %pad_maximum_fusion), channel_id=1, source_target_pairs={{0,8},{4,12},{8,0},{12,4},{1,9},{5,13},{9,1},{13,5},{2,10},{6,14},... | collective-permute-start | bytes 9224 | tf_op jit(solution)/shard_map/ppermute | solution.py:366
  6.1 4.1 %copy-start = (f32[16,16,128]{2,1,0:T(8,128)S(1)}, f32[16,16,128]{2,1,0:T(8,128)}, u32[]{:S(2)}) copy-start(f32[16,16,128]{2,1,0:T(8,128)} %refs_0_.1) | copy-start | bytes 393220

commit v5 on v4

--- a/solution.py
+++ b/solution.py
@@ -256,28 +256,17 @@
                 )
                 keep_first(out + embed, 4 * t + 3, halo - 1)
 
-        chunk = (pairs - 1) // 3
-        for start in range(0, pairs - 1, chunk):
+        for pair in range(pairs - 1):
             lhs = jnp.concatenate(
                 [
-                    jnp.concatenate(
-                        [
-                            first_ref[p + i, GRAIN * b : GRAIN * b + COLS, :]
-                            for b in range(3)
-                            for i in range(2)
-                        ],
-                        axis=1,
-                    )
-                    for p in range(start, start + chunk)
+                    first_ref[pair + i, GRAIN * b : GRAIN * b + COLS, :]
+                    for b in range(3)
+                    for i in range(2)
                 ],
-                axis=0,
+                axis=1,
             )
             out = jnp.dot(lhs, wm_ref[...], preferred_element_type=F32)
-            for i in range(chunk):
-                value = masked(
-                    half_silu(out[COLS * i : COLS * (i + 1)]), start + i, halo - 2
-                )
-                second_ref[start + i] = value.astype(BF16)
+            second_ref[pair] = masked(half_silu(out), pair, halo - 2).astype(BF16)
 
         new_count = count - 6
         new_tiles = pl.cdiv(new_count, 8)

time: 22.1 us -> 19.6 us (0.89)
  Pallas kernels: 13.3 us -> 10.8 us
    pallas_call x1, Pallas kernels: 11.8 us -> 9.2 us  [chain(): pl.pallas_call(body, out_shape=shape((1, channels, rows, cols), F32), in_...]
  transfers between devices with their start and end apart: 4 -> 4, of which waited for: 2 -> 2; matrix products, arithmetic and copies ran while one was open for 0% -> 0% of each run, Pallas kernels for 7% -> 8%
where the time goes in v5:
time: 19.6 us; the launch traced here: 19.4 us
  Pallas kernels  10.8 us (55%)
  waiting for transfers between devices  4.29 us (22%)
  starting transfers between devices  2.24 us (11%)
  between operations  1.35 us (7%)
  local copies, waits for them, and re-layouts  0.65 us (3%)
    pallas_call x1, Pallas kernels, chain(): pl.pallas_call(body, out_shape=shape((1, channels, rows, cols), F32), in_...  9.2 us
    ppermute x1, waiting for transfers between devices, chain(): two = lax.ppermute(both, 'tm', [(0, 2), (1, 3), (2, 0), (3, 1)])  2.51 us
    ppermute x1, waiting for transfers between devices, chain(): one = lax.ppermute(far, 'tm', [(0, 1), (1, 2), (2, 3), (3, 0)])  1.77 us
    ppermute x1, starting transfers between devices, chain(): after = lax.ppermute(start_noise, axes, moves(own, -1))  1.73 us
    pallas_call x1, Pallas kernels, chain(): pl.pallas_call(weights_kernel, out_shape=(pltpu.VMEM((384, 768), BF16), p...  1.57 us
    unnamed x4, local copies, waits for them, and re-layouts  0.64 us
    ppermute x1, starting transfers between devices, chain(): two = lax.ppermute(both, 'tm', [(0, 2), (1, 3), (2, 0), (3, 1)])  0.4 us
  transfers between devices with their start and end apart: 4, of which 2 were waited for; matrix products, arithmetic and copies ran while one was open for 0% of the time, Pallas kernels for 8%

profile of v5, /device:TPU:24, one launch (start us, length us, event | category | flops | bytes accessed | tf_op | source)
XLA Modules:
  0.0 19.4 jit_solution(10774549198576591770)
XLA Ops:
  1.3 0.0 copy-start.1
  1.3 0.6 %copy-done.1 = f32[1,128]{1,0:T(1,128)S(1)} copy-done((f32[1,128]{1,0:T(1,128)S(1)}, f32[1,128]{1,0:T(1,128)}, u32[]{:S(2)}) %copy-start.1) | copy-done | bytes 536
  2.0 0.1 collective-permute-start.2
  2.0 0.1 collective-permute-start
  2.1 1.7 %collective-permute-start.1 = (f32[16,16,128]{2,1,0:T(8,128)}, f32[16,16,128]{2,1,0:T(8,128)S(1)}, u32[]{:S(2)}, u32[]{:S(2)}) collective-permute-start(f32[16,16,128]{2,1,0:T(8,128)} %refs_0_.1), channel_id=1, source_target_pairs={{0,3},{1,0},{2,1},{3,2},{4,7},{5,4},{6,5},{7,6},{8,11},{9,8},{10,9... | collective-permute-start | bytes 393224 | tf_op jit(solution)/shard_map/ppermute | solution.py:352
  3.8 1.8 %collective-permute-done.2.refs_3_.refs_5_ = f32[3,128]{1,0:T(4,128)S(1)} collective-permute-done((f32[3,128]{1,0:T(4,128)S(1)}, f32[3,128]{1,0:T(4,128)S(1)}, u32[]{:S(2)}, u32[]{:S(2)}) %collective-permute-start.2) | collective-permute-done | bytes 1568 | tf_op jit(solution)/shard_map/ppermute | solution.py:353
  5.6 0.4 %collective-permute-start.3 = (f32[6,128]{1,0:T(8,128)S(1)}, f32[6,128]{1,0:T(8,128)S(1)}, u32[]{:S(2)}, u32[]{:S(2)}) collective-permute-start(f32[6,128]{1,0:T(8,128)S(1)} %pad_maximum_fusion), channel_id=1, source_target_pairs={{0,8},{4,12},{8,0},{12,4},{1,9},{5,13},{9,1},{13,5},{2,10},{6,14},... | collective-permute-start | bytes 9224 | tf_op jit(solution)/shard_map/ppermute | solution.py:355
  6.0 0.1 pad_add_fusion.refs_6_
  6.1 0.0 copy-start
  6.1 1.6 %shard_map.82 = (bf16[384,768]{1,0:T(8,128)(2,1)S(1)}, bf16[384,256]{1,0:T(8,128)(2,1)S(1)}, bf16[1536,256]{1,0:T(8,128)(2,1)S(1)}, bf16[1280,384]{1,0:T(8,128)(2,1)S(1)}, f32[1,128]{1,0:T(1,128)S(1)}) custom-call(bf16[9,16,128]{2,1,0:T(8,128)(2,1)} %bitcast.8, bf16[9,128,128]{2,1,0:T(8,128)(2,1)} %middle_ref.1, bf16[9,16,128]{2,1,0:T(8,128)(2,1)} %last_ref.1, ...), custom_call_target="tpu_custom_call" | custom-call | tf_op jit(solution)/shard_map/pallas_call | solution.py:358
  7.7 2.5 %collective-permute-done.3.refs_4_ = f32[6,128]{1,0:T(8,128)S(1)} collective-permute-done((f32[6,128]{1,0:T(8,128)S(1)}, f32[6,128]{1,0:T(8,128)S(1)}, u32[]{:S(2)}, u32[]{:S(2)}) %collective-permute-start.3) | collective-permute-done | bytes 3104 | tf_op jit(solution)/shard_map/ppermute | solution.py:355
  10.2 0.0 collective-permute-done.refs_1_
  10.2 0.0 collective-permute-done.1.refs_2_
  10.2 0.0 copy-done
  10.2 9.2 %shard_map.83 = f32[1,16,16,128]{3,2,1,0:T(8,128)} custom-call(f32[16,16,128]{2,1,0:T(8,128)S(1)} %copy-done, f32[16,16,128]{2,1,0:T(8,128)S(1)} %collective-permute-done.refs_1_, f32[16,16,128]{2,1,0:T(8,128)S(1)} %collective-permute-done.1.refs_2_, f32[3,128]{1,0:T(4,128)S(1)} %collective-permute-done.2.refs_3_.refs_5_, ...), custom_call_target="tpu_custom_call" | custom-call | tf_op jit(solution)/shard_map/pallas_call | solution.py:378
  (4 shorter events, 0.0 us)
Async XLA Ops:
  1.3 0.7 %copy-start.1 = (f32[1,128]{1,0:T(1,128)S(1)}, f32[1,128]{1,0:T(1,128)}, u32[]{:S(2)}) copy-start(f32[1,128]{1,0:T(1,128)} %param.9) | copy-start | bytes 1540
  2.0 3.6 %collective-permute-start.2 = (f32[3,128]{1,0:T(4,128)S(1)}, f32[3,128]{1,0:T(4,128)S(1)}, u32[]{:S(2)}, u32[]{:S(2)}) collective-permute-start(f32[3,128]{1,0:T(4,128)S(1)} %pad_maximum_fusion.1), channel_id=1, source_target_pairs={{0,4},{4,8},{8,12},{12,0},{1,5},{5,9},{9,13},{13,1},{2,6},{6,10},{... | collective-permute-start | bytes 4616 | tf_op jit(solution)/shard_map/ppermute | solution.py:353
  2.0 8.2 %collective-permute-start = (f32[16,16,128]{2,1,0:T(8,128)}, f32[16,16,128]{2,1,0:T(8,128)S(1)}, u32[]{:S(2)}, u32[]{:S(2)}) collective-permute-start(f32[16,16,128]{2,1,0:T(8,128)} %refs_0_.1), channel_id=1, source_target_pairs={{0,1},{1,2},{2,3},{3,0},{4,5},{5,6},{6,7},{7,4},{8,9},{9,10},{10,1... | collective-permute-start | bytes 393224 | tf_op jit(solution)/shard_map/ppermute | solution.py:351
  2.1 8.1 %collective-permute-start.1 = (f32[16,16,128]{2,1,0:T(8,128)}, f32[16,16,128]{2,1,0:T(8,128)S(1)}, u32[]{:S(2)}, u32[]{:S(2)}) collective-permute-start(f32[16,16,128]{2,1,0:T(8,128)} %refs_0_.1), channel_id=1, source_target_pairs={{0,3},{1,0},{2,1},{3,2},{4,7},{5,4},{6,5},{7,6},{8,11},{9,8},{10,9... | collective-permute-start | bytes 393224 | tf_op jit(solution)/shard_map/ppermute | solution.py:352
  5.6 4.6 %collective-permute-start.3 = (f32[6,128]{1,0:T(8,128)S(1)}, f32[6,128]{1,0:T(8,128)S(1)}, u32[]{:S(2)}, u32[]{:S(2)}) collective-permute-start(f32[6,128]{1,0:T(8,128)S(1)} %pad_maximum_fusion), channel_id=1, source_target_pairs={{0,8},{4,12},{8,0},{12,4},{1,9},{5,13},{9,1},{13,5},{2,10},{6,14},... | collective-permute-start | bytes 9224 | tf_op jit(solution)/shard_map/ppermute | solution.py:355
  6.1 4.1 %copy-start = (f32[16,16,128]{2,1,0:T(8,128)S(1)}, f32[16,16,128]{2,1,0:T(8,128)}, u32[]{:S(2)}) copy-start(f32[16,16,128]{2,1,0:T(8,128)} %refs_0_.1) | copy-start | bytes 393220

commit v6 on v5

--- a/solution.py
+++ b/solution.py
@@ -79,38 +79,47 @@
 
 
 def weights_kernel(
-    first_ref, middle_ref, last_ref, bias_in_ref, w1a_ref, w1b_ref, wm_ref, w3_ref, bias_ref
+    first_ref, middle_ref, last_ref, bias_in_ref, w1_ref, wm_ref, w3_ref, bias_ref
 ):
     bias_ref[...] = jnp.concatenate([bias_in_ref[...]] * 8, axis=1)
-    w1a_ref[...] = jnp.zeros(w1a_ref.shape, BF16)
-    w1b_ref[...] = jnp.zeros(w1b_ref.shape, BF16)
+    halves = [first_ref[tap] * BF16(0.5) for tap in range(9)]
+    none = jnp.zeros((16, 128), BF16)
+    for place in range(4):
+        for lanes in range(8):
+            k = (lanes - 2 * place) % 8
+            for out in range(2):
+                for part in range(2):
+                    a = k % 4 - out
+                    b = 2 if part else k // 4
+                    used = 0 <= a < 3 and not (part and k >= 4)
+                    w1_ref[
+                        place,
+                        pl.ds(128 * part + 16 * lanes, 16),
+                        pl.ds(128 * out, 128),
+                    ] = halves[3 * a + b] if used else none
+    zero = jnp.zeros((128, 128), BF16)
     for tap in range(9):
         a, b = divmod(tap, 3)
-        block = first_ref[tap] * BF16(0.5)
-        for out in range(6):
-            row = out + a
-            w1a_ref[pl.ds(128 * b + 16 * row, 16), pl.ds(128 * out, 128)] = block
-        for out in range(2):
-            row = 6 + out + a
-            place = row - 8 if row >= 8 else row
-            w1b_ref[pl.ds(128 * b + 16 * place, 16), pl.ds(128 * out, 128)] = block
         block = (middle_ref[tap].astype(F32).T * 0.5).astype(BF16)
         for out in range(2):
             wm_ref[pl.ds(512 * b + 128 * (out + a), 128), pl.ds(128 * out, 128)] = block
-    zero = jnp.zeros((128, 128), BF16)
     for b in range(3):
         wm_ref[pl.ds(512 * b + 384, 128), pl.ds(0, 128)] = zero
         wm_ref[pl.ds(512 * b, 128), pl.ds(128, 128)] = zero
-        for row in range(10):
-            parts = []
-            for out in range(8):
-                a = row - out
-                if 0 <= a < 3:
-                    parts.append(last_ref[3 * a + b].astype(F32))
-                else:
-                    parts.append(jnp.zeros((16, 128), F32))
-            block = jnp.concatenate(parts, axis=0).T.astype(BF16)
-            w3_ref[pl.ds(128 * row, 128), pl.ds(128 * b, 128)] = block
+    for place in range(4):
+        for row in range(2):
+            for part in range(2):
+                parts = []
+                for lanes in range(8):
+                    k = (lanes - 2 * (place - 1)) % 8
+                    a = row + 2 - k % 4
+                    b = 2 if part else k // 4
+                    if 0 <= a < 3 and not (part and k >= 4):
+                        parts.append(last_ref[3 * a + b].astype(F32))
+                    else:
+                        parts.append(jnp.zeros((16, 128), F32))
+                block = jnp.concatenate(parts, axis=0).T.astype(BF16)
+                w3_ref[place, pl.ds(128 * row, 128), pl.ds(128 * part, 128)] = block
 
 
 def split3(value):
@@ -144,13 +153,13 @@
     three_ref,
     place_ref,
     bias_ref,
-    w1a_ref,
-    w1b_ref,
+    w1_ref,
     wm_ref,
     w3_ref,
     out_ref,
     state_ref,
     zb_ref,
+    zr_ref,
     first_ref,
     second_ref,
 ):
@@ -199,7 +208,11 @@
             state_ref[t] = moved * lane_scale(t, halo)
 
     bias = bias_ref[...]
-    params = [two_ref[3:6], two_ref[0:3], one_ref[...]]
+    params = [
+        three_ref[...],
+        two_ref[...],
+        jnp.where(time == 2, three_ref[...], one_ref[...]),
+    ]
 
     def masked(value, pair, margin):
         halves = []
@@ -227,34 +240,33 @@
         keep = params[step][1:2]
         rate = params[step][2:3]
 
+        def padded_tile(ref, t, z):
+            ref[t, GRAIN : GRAIN + COLS, :] = z.astype(BF16)
+            ref[t, 0:GRAIN, :] = shifted_rows(z[COLS - GRAIN :], 1).astype(BF16)
+            ref[t, GRAIN + COLS :, :] = shifted_rows(z[:GRAIN], -1).astype(BF16)
+
         for t in range(tiles):
-            z = state_ref[t]
-            zb_ref[t, GRAIN : GRAIN + COLS, :] = z.astype(BF16)
-            zb_ref[t, 0:GRAIN, :] = shifted_rows(z[COLS - GRAIN :], 1).astype(BF16)
-            zb_ref[t, GRAIN + COLS :, :] = shifted_rows(z[:GRAIN], -1).astype(BF16)
-
-        def three(t):
-            return jnp.concatenate(
-                [zb_ref[t, GRAIN * b : GRAIN * b + COLS, :] for b in range(3)], axis=1
+            padded_tile(zb_ref, t, state_ref[t])
+            padded_tile(zr_ref, t, pltpu.roll(state_ref[t], 64, 1))
+
+        for pair in range(pairs):
+            t, place = divmod(pair, 4)
+            here = [zb_ref[t, GRAIN * b : GRAIN * b + COLS, :] for b in range(3)]
+            turned = zr_ref[t, GRAIN : GRAIN + COLS, :]
+            if place < 3:
+                window = (lane >= 32 * place) & (lane < 32 * place + 64)
+                lhs = [jnp.where(window, here[0], turned), here[2]]
+            else:
+                after = [zb_ref[t + 1, GRAIN * b : GRAIN * b + COLS, :] for b in (0, 2)]
+                mixed = jnp.where(lane < 64, turned, zr_ref[t + 1, GRAIN : GRAIN + COLS, :])
+                lhs = [
+                    jnp.where(lane < 32, after[0], jnp.where(lane < 96, mixed, here[0])),
+                    jnp.where(lane < 64, after[1], here[2]),
+                ]
+            out = jnp.dot(
+                jnp.concatenate(lhs, axis=1), w1_ref[place], preferred_element_type=F32
             )
-
-        for t in range(tiles):
-            here = min(3, pairs - 4 * t)
-            if here > 0:
-                out = jnp.dot(
-                    three(t), w1a_ref[:, : 256 * here], preferred_element_type=F32
-                )
-                for i in range(here):
-                    value = out[:, 256 * i : 256 * (i + 1)] + embed
-                    keep_first(value, 4 * t + i, halo - 1)
-            if 4 * t + 3 < pairs:
-                both = jnp.concatenate([lane < 64] * 3, axis=1)
-                out = jnp.dot(
-                    jnp.where(both, three(t + 1), three(t)),
-                    w1b_ref[...],
-                    preferred_element_type=F32,
-                )
-                keep_first(out + embed, 4 * t + 3, halo - 1)
+            keep_first(out + embed, pair, halo - 1)
 
         for pair in range(pairs - 1):
             lhs = jnp.concatenate(
@@ -268,27 +280,37 @@
             out = jnp.dot(lhs, wm_ref[...], preferred_element_type=F32)
             second_ref[pair] = masked(half_silu(out), pair, halo - 2).astype(BF16)
 
-        new_count = count - 6
-        new_tiles = pl.cdiv(new_count, 8)
-        for i in range(pairs - 1, 4 * new_tiles + 1):
-            second_ref[i] = jnp.zeros((COLS, 256), BF16)
-        lhs = jnp.concatenate(
-            [
-                jnp.concatenate([second_ref[4 * t + i] for i in range(5)], axis=1)
-                for t in range(new_tiles)
-            ],
-            axis=0,
-        )
-        out = jnp.dot(lhs, w3_ref[...], preferred_element_type=F32)
-        for t in range(new_tiles):
-            g = out[COLS * t : COLS * (t + 1)]
-            left = g[:, 0:128]
-            right = g[:, 256:384]
+        reach = [
+            jnp.dot(second_ref[pair], w3_ref[pair % 4], preferred_element_type=F32)
+            for pair in range(pairs - 1)
+        ]
+        low = lane < 64
+
+        def spread(t, part):
+            got = [
+                reach[p][:, COLS * part : COLS * (part + 1)]
+                if p < pairs - 1
+                else jnp.zeros((COLS, COLS), F32)
+                for p in range(4 * t, 4 * t + 5)
+            ]
+            proper = jnp.where(low, got[1], got[3]) + jnp.where(
+                lane < 32, got[0], jnp.where(lane < 96, got[2], got[4])
+            )
+            if part == 1:
+                return proper, None
+            other = jnp.where(low, got[3], got[1]) + jnp.where(
+                (lane < 32) | (lane >= 96), got[2], jnp.where(low, got[4], got[0])
+            )
+            return proper, pltpu.roll(other, 64, 1)
+
+        for t in range(pl.cdiv(count - 6, 8)):
+            left, centre = spread(t, 0)
+            right, _ = spread(t, 1)
             left = jnp.concatenate(
                 [shifted_rows(left[COLS - GRAIN :], 1), left[: COLS - GRAIN]], axis=0
             )
             right = jnp.concatenate([right[GRAIN:], shifted_rows(right[:GRAIN], -1)], axis=0)
-            conv = left + g[:, 128:256] + right
+            conv = left + centre + right
             here = state_ref[t]
             old = jnp.concatenate([here[:, 48:], state_ref[t + 1][:, :48]], axis=1) if (
                 t + 1 < tiles
@@ -350,22 +372,21 @@
     own = [(t, t) for t in range(tm_size)]
     before = lax.ppermute(start_noise, axes, moves(own, 1))
     after = lax.ppermute(start_noise, axes, moves(own, -1))
-    one = lax.ppermute(far, "tm", [(0, 1), (1, 2), (2, 3), (3, 0)])
-    both = jnp.concatenate([far, one], axis=0)
-    two = lax.ppermute(both, "tm", [(0, 2), (1, 3), (2, 0), (3, 1)])
-    three = one
-
-    w1a, w1b, wm, w3, bias = pl.pallas_call(
+    def exchanged(apart):
+        return lax.ppermute(far, "tm", [(t, t ^ apart) for t in range(tm_size)])
+
+    one, two, three = (exchanged(apart) for apart in (1, 2, 3))
+
+    w1, wm, w3, bias = pl.pallas_call(
         weights_kernel,
         out_shape=(
-            pltpu.VMEM((384, 768), BF16),
-            pltpu.VMEM((384, 256), BF16),
+            pltpu.VMEM((4, 256, 256), BF16),
             pltpu.VMEM((1536, 256), BF16),
-            pltpu.VMEM((1280, 384), BF16),
+            pltpu.VMEM((4, 256, 256), BF16),
             pltpu.VMEM((1, COLS), F32),
         ),
         in_specs=[vmem] * 4,
-        out_specs=(vmem,) * 5,
+        out_specs=(vmem,) * 4,
     )(jnp.swapaxes(conv_first, 1, 2), conv_middle, conv_last, out_bias.reshape(1, channels))
 
     place = jnp.stack([lax.axis_index("tm"), lax.axis_index("space")]).astype(jnp.int32)
@@ -378,16 +399,17 @@
     return pl.pallas_call(
         body,
         out_shape=shape((1, channels, rows, cols), F32),
-        in_specs=[vmem] * 6 + [smem] + [vmem] * 5,
+        in_specs=[vmem] * 6 + [smem] + [vmem] * 4,
         out_specs=vmem,
         scratch_shapes=[
             pltpu.VMEM((pl.cdiv(total, 8), COLS, COLS), F32),
             pltpu.VMEM((pl.cdiv(total, 8), PAD, COLS), BF16),
+            pltpu.VMEM((pl.cdiv(total, 8), PAD, COLS), BF16),
             pltpu.VMEM((pairs, PAD, 256), BF16),
-            pltpu.VMEM((pairs + 1, COLS, 256), BF16),
+            pltpu.VMEM((pairs - 1, COLS, 256), BF16),
         ],
         compiler_params=pltpu.CompilerParams(vmem_limit_bytes=48 << 20),
-    )(start_noise, before, after, one, two, three, place, bias, w1a, w1b, wm, w3)
+    )(start_noise, before, after, one, two, three, place, bias, w1, wm, w3)
 
 
 def solution(mesh):

time: 19.6 us -> 18.3 us (0.934)
  waiting for transfers between devices: 4.29 us -> 0.06 us
  starting transfers between devices: 2.24 us -> 6.13 us
  Pallas kernels: 10.8 us -> 9.68 us
    ppermute x2 -> x3, waiting for transfers between devices: 4.28 us -> 0.05 us  [exchanged(): return lax.ppermute(far, 'tm', [(t, t ^ apart) for t in range(tm_size)])]
    ppermute x2 -> x3, starting transfers between devices: 0.45 us -> 4.39 us  [exchanged(): return lax.ppermute(far, 'tm', [(t, t ^ apart) for t in range(tm_size)])]
    pallas_call x1, Pallas kernels: 9.2 us -> 8.27 us  [chain(): pl.pallas_call(body, out_shape=shape((1, channels, rows, cols), F32), in_...]
  transfers between devices with their start and end apart: 4 -> 5, of which waited for: 2 -> 0; matrix products, arithmetic and copies ran while one was open for 0% -> 2% of each run, Pallas kernels for 8% -> 8%
where the time goes in v6:
time: 18.3 us; the launch traced here: 18.1 us
  Pallas kernels  9.68 us (53%)
  starting transfers between devices  6.13 us (33%)
  between operations  1.33 us (7%)
  local copies, waits for them, and re-layouts  0.73 us (4%)
    pallas_call x1, Pallas kernels, chain(): pl.pallas_call(body, out_shape=shape((1, channels, rows, cols), F32), in_...  8.27 us
    ppermute x3, starting transfers between devices, exchanged(): return lax.ppermute(far, 'tm', [(t, t ^ apart) for t in range(tm_size)])  4.39 us
    ppermute x1, starting transfers between devices, chain(): after = lax.ppermute(start_noise, axes, moves(own, -1))  1.74 us
    pallas_call x1, Pallas kernels, chain(): pl.pallas_call(weights_kernel, out_shape=(pltpu.VMEM((4, 256, 256), BF16)...  1.41 us
    unnamed x4, local copies, waits for them, and re-layouts  0.58 us
  transfers between devices with their start and end apart: 5, of which 0 were waited for; matrix products, arithmetic and copies ran while one was open for 2% of the time, Pallas kernels for 8%

profile of v6, /device:TPU:24, one launch (start us, length us, event | category | flops | bytes accessed | tf_op | source)
XLA Modules:
  0.0 18.1 jit_solution(10610920995645506638)
XLA Ops:
  0.0 0.0 collective-permute-start
  0.0 1.7 %collective-permute-start.1 = (f32[16,16,128]{2,1,0:T(8,128)}, f32[16,16,128]{2,1,0:T(8,128)S(1)}, u32[]{:S(2)}, u32[]{:S(2)}) collective-permute-start(f32[16,16,128]{2,1,0:T(8,128)} %refs_0_.1), channel_id=1, source_target_pairs={{0,3},{1,0},{2,1},{3,2},{4,7},{5,4},{6,5},{7,6},{8,11},{9,8},{10,9... | collective-permute-start | bytes 393224 | tf_op jit(solution)/shard_map/ppermute | solution.py:374
  3.0 0.1 pad.3.clone
  3.1 0.0 copy-start.1
  3.1 0.1 pad.4.clone
  3.2 0.6 %copy-done.1 = f32[1,128]{1,0:T(1,128)S(1)} copy-done((f32[1,128]{1,0:T(1,128)S(1)}, f32[1,128]{1,0:T(1,128)}, u32[]{:S(2)}) %copy-start.1) | copy-done | bytes 536
  3.8 0.1 maximum_maximum_fusion
  3.8 0.0 collective-permute-start.4
  3.9 1.9 %collective-permute-start.3 = (f32[3,128]{1,0:T(4,128)S(1)}, f32[3,128]{1,0:T(4,128)S(1)}, u32[]{:S(2)}, u32[]{:S(2)}) collective-permute-start(f32[3,128]{1,0:T(4,128)S(1)} %maximum_maximum_fusion), channel_id=1, source_target_pairs={{0,8},{4,12},{8,0},{12,4},{1,9},{5,13},{9,1},{13,5},{2,10},{6,14},... | collective-permute-start | bytes 4616 | tf_op jit(solution)/shard_map/ppermute | solution.py:376
  5.8 2.5 %collective-permute-start.2 = (f32[3,128]{1,0:T(4,128)S(1)}, f32[3,128]{1,0:T(4,128)S(1)}, u32[]{:S(2)}, u32[]{:S(2)}) collective-permute-start(f32[3,128]{1,0:T(4,128)S(1)} %maximum_maximum_fusion), channel_id=1, source_target_pairs={{0,4},{4,0},{8,12},{12,8},{1,5},{5,1},{9,13},{13,9},{2,6},{6,2},{1... | collective-permute-start | bytes 4616 | tf_op jit(solution)/shard_map/ppermute | solution.py:376
  8.2 0.1 pad_add_fusion.refs_6_
  8.3 0.0 copy-start
  8.3 1.4 %shard_map.82 = (bf16[4,256,256]{2,1,0:T(8,128)(2,1)S(1)}, bf16[1536,256]{1,0:T(8,128)(2,1)S(1)}, bf16[4,256,256]{2,1,0:T(8,128)(2,1)S(1)}, f32[1,128]{1,0:T(1,128)S(1)}) custom-call(bf16[9,16,128]{2,1,0:T(8,128)(2,1)} %bitcast.6, bf16[9,128,128]{2,1,0:T(8,128)(2,1)} %middle_ref.1, bf16[9,16,128]{2,1,0:T(8,128)(2,1)} %last_ref.1, f32[1,16]{1,0:T(1,128)} %bitcast.7), custom_call_target="tpu_custom_call" | custom-call | tf_op jit(solution)/shard_map/pallas_call | solution.py:380
  9.7 0.0 collective-permute-done.4.refs_5_
  9.7 0.0 collective-permute-done.3.refs_4_
  9.8 0.0 collective-permute-done.2.refs_3_
  9.8 0.0 collective-permute-done.refs_1_
  9.8 0.0 collective-permute-done.1.refs_2_
  9.8 0.0 copy-done
  9.8 8.3 %shard_map.83 = f32[1,16,16,128]{3,2,1,0:T(8,128)} custom-call(f32[16,16,128]{2,1,0:T(8,128)S(1)} %copy-done, f32[16,16,128]{2,1,0:T(8,128)S(1)} %collective-permute-done.refs_1_, f32[16,16,128]{2,1,0:T(8,128)S(1)} %collective-permute-done.1.refs_2_, f32[3,128]{1,0:T(4,128)S(1)} %collective-permute-done.2.refs_3_, ...), custom_call_target="tpu_custom_call" | custom-call | tf_op jit(solution)/shard_map/pallas_call | solution.py:399
Async XLA Ops:
  0.0 9.8 %collective-permute-start = (f32[16,16,128]{2,1,0:T(8,128)}, f32[16,16,128]{2,1,0:T(8,128)S(1)}, u32[]{:S(2)}, u32[]{:S(2)}) collective-permute-start(f32[16,16,128]{2,1,0:T(8,128)} %refs_0_.1), channel_id=1, source_target_pairs={{0,1},{1,2},{2,3},{3,0},{4,5},{5,6},{6,7},{7,4},{8,9},{9,10},{10,1... | collective-permute-start | bytes 393224 | tf_op jit(solution)/shard_map/ppermute | solution.py:373
  0.0 9.8 %collective-permute-start.1 = (f32[16,16,128]{2,1,0:T(8,128)}, f32[16,16,128]{2,1,0:T(8,128)S(1)}, u32[]{:S(2)}, u32[]{:S(2)}) collective-permute-start(f32[16,16,128]{2,1,0:T(8,128)} %refs_0_.1), channel_id=1, source_target_pairs={{0,3},{1,0},{2,1},{3,2},{4,7},{5,4},{6,5},{7,6},{8,11},{9,8},{10,9... | collective-permute-start | bytes 393224 | tf_op jit(solution)/shard_map/ppermute | solution.py:374
  3.1 0.7 %copy-start.1 = (f32[1,128]{1,0:T(1,128)S(1)}, f32[1,128]{1,0:T(1,128)}, u32[]{:S(2)}) copy-start(f32[1,128]{1,0:T(1,128)} %param.9) | copy-start | bytes 1540
  3.8 5.9 %collective-permute-start.4 = (f32[3,128]{1,0:T(4,128)S(1)}, f32[3,128]{1,0:T(4,128)S(1)}, u32[]{:S(2)}, u32[]{:S(2)}) collective-permute-start(f32[3,128]{1,0:T(4,128)S(1)} %maximum_maximum_fusion), channel_id=1, source_target_pairs={{0,12},{4,8},{8,4},{12,0},{1,13},{5,9},{9,5},{13,1},{2,14},{6,10},... | collective-permute-start | bytes 4616 | tf_op jit(solution)/shard_map/ppermute | solution.py:376
  3.9 5.9 %collective-permute-start.3 = (f32[3,128]{1,0:T(4,128)S(1)}, f32[3,128]{1,0:T(4,128)S(1)}, u32[]{:S(2)}, u32[]{:S(2)}) collective-permute-start(f32[3,128]{1,0:T(4,128)S(1)} %maximum_maximum_fusion), channel_id=1, source_target_pairs={{0,8},{4,12},{8,0},{12,4},{1,9},{5,13},{9,1},{13,5},{2,10},{6,14},... | collective-permute-start | bytes 4616 | tf_op jit(solution)/shard_map/ppermute | solution.py:376
  5.8 4.0 %collective-permute-start.2 = (f32[3,128]{1,0:T(4,128)S(1)}, f32[3,128]{1,0:T(4,128)S(1)}, u32[]{:S(2)}, u32[]{:S(2)}) collective-permute-start(f32[3,128]{1,0:T(4,128)S(1)} %maximum_maximum_fusion), channel_id=1, source_target_pairs={{0,4},{4,0},{8,12},{12,8},{1,5},{5,1},{9,13},{13,9},{2,6},{6,2},{1... | collective-permute-start | bytes 4616 | tf_op jit(solution)/shard_map/ppermute | solution.py:376
  8.3 1.5 %copy-start = (f32[16,16,128]{2,1,0:T(8,128)S(1)}, f32[16,16,128]{2,1,0:T(8,128)}, u32[]{:S(2)}) copy-start(f32[16,16,128]{2,1,0:T(8,128)} %refs_0_.1) | copy-start | bytes 393220

commit v7 on v6

--- a/solution.py
+++ b/solution.py
@@ -76,6 +76,12 @@
 COLS = 128
 GRAIN = 16
 PAD = COLS + 2 * GRAIN
+
+
+def pack_kernel(embed_ref, keep_ref, rate_ref, out_ref):
+    out_ref[0:1] = embed_ref[...]
+    out_ref[1:2] = jnp.broadcast_to(keep_ref[...], (1, COLS))
+    out_ref[2:3] = jnp.broadcast_to(rate_ref[...], (1, COLS))
 
 
 def weights_kernel(
@@ -146,12 +152,11 @@
     space_size,
     rows,
     noise_ref,
-    before_ref,
-    after_ref,
+    two_ref,
+    near_ref,
+    across_ref,
     one_ref,
-    two_ref,
     three_ref,
-    place_ref,
     bias_ref,
     w1_ref,
     wm_ref,
@@ -163,8 +168,9 @@
     first_ref,
     second_ref,
 ):
-    time = place_ref[0]
-    tile = place_ref[1]
+    time = lax.axis_index("tm")
+    tile = lax.axis_index("space")
+    even = tile % 2 == 0
     top = (tile > 0).astype(F32)
     bottom = (tile < space_size - 1).astype(F32)
 
@@ -191,11 +197,13 @@
             parts = []
             for e in range(8 * t, 8 * t + 8):
                 if e < halo:
-                    parts.append(before_ref[:, rows - halo + e, :])
+                    row = rows - halo + e
+                    parts.append(jnp.where(even, across_ref[:, row, :], near_ref[:, row, :]))
                 elif e < halo + rows:
                     parts.append(noise_ref[:, e - halo, :])
                 elif e < total:
-                    parts.append(after_ref[:, e - halo - rows, :])
+                    row = e - halo - rows
+                    parts.append(jnp.where(even, near_ref[:, row, :], across_ref[:, row, :]))
                 else:
                     parts.append(jnp.zeros((16, COLS), F32))
             block = jnp.concatenate(parts, axis=0)
@@ -349,33 +357,29 @@
     tm_size = lax.axis_size("tm")
     space_size = lax.axis_size("space")
     vmem = pl.BlockSpec(memory_space=pltpu.VMEM)
-    smem = pl.BlockSpec(memory_space=pltpu.SMEM)
     shape = jax.ShapeDtypeStruct
 
-    far = jnp.concatenate(
-        [
-            time_embed,
-            jnp.broadcast_to(keep_rate[:, None], (1, cols)),
-            jnp.broadcast_to(denoise_rate[:, None], (1, cols)),
-        ],
-        axis=0,
-    )
-
-    def moves(times, tiles):
-        return [
-            (t * space_size + s, u * space_size + (s + tiles) % space_size)
-            for t, u in times
-            for s in range(space_size)
-        ]
-
-    axes = ("tm", "space")
-    own = [(t, t) for t in range(tm_size)]
-    before = lax.ppermute(start_noise, axes, moves(own, 1))
-    after = lax.ppermute(start_noise, axes, moves(own, -1))
+    far = pl.pallas_call(
+        pack_kernel,
+        out_shape=pltpu.VMEM((3, cols), F32),
+        in_specs=[vmem] * 3,
+        out_specs=vmem,
+    )(time_embed, keep_rate.reshape(1, 1), denoise_rate.reshape(1, 1))
+
+    def swapped(value, first):
+        pairs = [(i, i + 1) for i in range(first, space_size - 1, 2)]
+        pairs += [(0, space_size - 1)] if first else []
+        return lax.ppermute(value, "space", pairs + [(j, i) for i, j in pairs])
+
     def exchanged(apart):
         return lax.ppermute(far, "tm", [(t, t ^ apart) for t in range(tm_size)])
 
-    one, two, three = (exchanged(apart) for apart in (1, 2, 3))
+    start_noise, far = lax.optimization_barrier((start_noise, far))
+    two = exchanged(2)
+    near = swapped(start_noise, 0)
+    across = swapped(start_noise, 1)
+    one = exchanged(1)
+    three = exchanged(3)
 
     w1, wm, w3, bias = pl.pallas_call(
         weights_kernel,
@@ -389,7 +393,6 @@
         out_specs=(vmem,) * 4,
     )(jnp.swapaxes(conv_first, 1, 2), conv_middle, conv_last, out_bias.reshape(1, channels))
 
-    place = jnp.stack([lax.axis_index("tm"), lax.axis_index("space")]).astype(jnp.int32)
     total = rows + 2 * HALO
     pairs = (total - 2) // 2
 
@@ -399,7 +402,7 @@
     return pl.pallas_call(
         body,
         out_shape=shape((1, channels, rows, cols), F32),
-        in_specs=[vmem] * 6 + [smem] + [vmem] * 4,
+        in_specs=[vmem] * 10,
         out_specs=vmem,
         scratch_shapes=[
             pltpu.VMEM((pl.cdiv(total, 8), COLS, COLS), F32),
@@ -409,7 +412,7 @@
             pltpu.VMEM((pairs - 1, COLS, 256), BF16),
         ],
         compiler_params=pltpu.CompilerParams(vmem_limit_bytes=48 << 20),
-    )(start_noise, before, after, one, two, three, place, bias, w1, wm, w3)
+    )(start_noise, two, near, across, one, three, bias, w1, wm, w3)
 
 
 def solution(mesh):
@@ -424,7 +427,9 @@
         P(),
     )
     return jax.shard_map(
-        chain if mesh.shape["tm"] == ITERS + 1 else picard,
+        chain
+        if mesh.shape["tm"] == ITERS + 1 and mesh.shape["space"] % 2 == 0
+        else picard,
         mesh=mesh,
         in_specs=placed,
         out_specs=P("tm", None, ("groups", "space"), None),

time: 18.3 us -> 17.5 us (0.956)
  local copies, waits for them, and re-layouts: 0.73 us -> 0.01 us
  Pallas kernels: 9.68 us -> 9.9 us
    pallas_call x0 -> x1, Pallas kernels: none -> 0.73 us  [chain(): pl.pallas_call(pack_kernel, out_shape=pltpu.VMEM((3, cols), F32), in_spec...]
    unnamed x4 -> x2, local copies, waits for them, and re-layouts: 0.58 us -> 0.01 us
    pallas_call x1, Pallas kernels: 8.27 us -> 7.77 us  [chain(): pl.pallas_call(body, out_shape=shape((1, channels, rows, cols), F32), in_...]
  transfers between devices with their start and end apart: 5 -> 5, of which waited for: 0 -> 1; matrix products, arithmetic and copies ran while one was open for 2% -> 0% of each run, Pallas kernels for 8% -> 8%
where the time goes in v7:
time: 17.5 us; the launch traced here: 17.4 us
  Pallas kernels  9.9 us (57%)
  starting transfers between devices  5.99 us (34%)
  between operations  1.33 us (8%)
    pallas_call x1, Pallas kernels, chain(): pl.pallas_call(body, out_shape=shape((1, channels, rows, cols), F32), in_...  7.77 us
    ppermute x3, starting transfers between devices, exchanged(): return lax.ppermute(far, 'tm', [(t, t ^ apart) for t in range(tm_size)])  4.39 us
    ppermute x2, starting transfers between devices, swapped(): return lax.ppermute(value, 'space', pairs + [(j, i) for i, j in pairs])  1.61 us
    pallas_call x1, Pallas kernels, chain(): pl.pallas_call(weights_kernel, out_shape=(pltpu.VMEM((4, 256, 256), BF16)...  1.41 us
    pallas_call x1, Pallas kernels, chain(): pl.pallas_call(pack_kernel, out_shape=pltpu.VMEM((3, cols), F32), in_spec...  0.73 us
  transfers between devices with their start and end apart: 5, of which 1 were waited for; matrix products, arithmetic and copies ran while one was open for 0% of the time, Pallas kernels for 8%

profile of v7, /device:TPU:24, one launch (start us, length us, event | category | flops | bytes accessed | tf_op | source)
XLA Modules:
  0.0 17.4 jit_solution(15470314734402845750)
XLA Ops:
  1.3 0.7 %shard_map.82 = f32[3,128]{1,0:T(4,128)S(1)} custom-call(f32[1,128]{1,0:T(1,128)} %embed_ref.1, f32[1,1]{1,0:T(1,128)} %bitcast.4.keep_ref, f32[1,1]{1,0:T(1,128)} %bitcast.5.rate_ref), custom_call_target="tpu_custom_call" | custom-call | tf_op jit(solution)/shard_map/pallas_call | solution.py:362
  2.0 0.9 %collective-permute-start.2 = (f32[16,16,128]{2,1,0:T(8,128)}, f32[16,16,128]{2,1,0:T(8,128)S(1)}, u32[]{:S(2)}, u32[]{:S(2)}) collective-permute-start(f32[16,16,128]{2,1,0:T(8,128)} %refs_0_), channel_id=1, source_target_pairs={{1,2},{0,3},{2,1},{3,0},{5,6},{4,7},{6,5},{7,4},{9,10},{8,11},{10,... | collective-permute-start | bytes 393224 | tf_op jit(solution)/shard_map/ppermute | solution.py:372
  3.0 0.7 %collective-permute-start.1 = (f32[16,16,128]{2,1,0:T(8,128)}, f32[16,16,128]{2,1,0:T(8,128)S(1)}, u32[]{:S(2)}, u32[]{:S(2)}) collective-permute-start(f32[16,16,128]{2,1,0:T(8,128)} %refs_0_), channel_id=1, source_target_pairs={{0,1},{2,3},{1,0},{3,2},{4,5},{6,7},{5,4},{7,6},{8,9},{10,11},{9,8... | collective-permute-start | bytes 393224 | tf_op jit(solution)/shard_map/ppermute | solution.py:372
  3.6 0.2 %collective-permute-start.4 = (f32[3,128]{1,0:T(4,128)S(1)}, f32[3,128]{1,0:T(4,128)S(1)}, u32[]{:S(2)}, u32[]{:S(2)}) collective-permute-start(f32[3,128]{1,0:T(4,128)S(1)} %shard_map.82), channel_id=1, source_target_pairs={{0,12},{4,8},{8,4},{12,0},{1,13},{5,9},{9,5},{13,1},{2,14},{6,10},... | collective-permute-start | bytes 4616 | tf_op jit(solution)/shard_map/ppermute | solution.py:375
  3.9 0.7 %collective-permute-start.3 = (f32[3,128]{1,0:T(4,128)S(1)}, f32[3,128]{1,0:T(4,128)S(1)}, u32[]{:S(2)}, u32[]{:S(2)}) collective-permute-start(f32[3,128]{1,0:T(4,128)S(1)} %shard_map.82), channel_id=1, source_target_pairs={{0,4},{4,0},{8,12},{12,8},{1,5},{5,1},{9,13},{13,9},{2,6},{6,2},{1... | collective-permute-start | bytes 4616 | tf_op jit(solution)/shard_map/ppermute | solution.py:375
  4.5 3.5 %collective-permute-start = (f32[3,128]{1,0:T(4,128)S(1)}, f32[3,128]{1,0:T(4,128)S(1)}, u32[]{:S(2)}, u32[]{:S(2)}) collective-permute-start(f32[3,128]{1,0:T(4,128)S(1)} %shard_map.82), channel_id=1, source_target_pairs={{0,8},{4,12},{8,0},{12,4},{1,9},{5,13},{9,1},{13,5},{2,10},{6,14},... | collective-permute-start | bytes 4616 | tf_op jit(solution)/shard_map/ppermute | solution.py:375
  8.0 0.0 copy-start
  8.0 1.4 %shard_map.83 = (bf16[4,256,256]{2,1,0:T(8,128)(2,1)S(1)}, bf16[1536,256]{1,0:T(8,128)(2,1)S(1)}, bf16[4,256,256]{2,1,0:T(8,128)(2,1)S(1)}, f32[1,128]{1,0:T(1,128)S(1)}) custom-call(bf16[9,16,128]{2,1,0:T(8,128)(2,1)} %bitcast.6, bf16[9,128,128]{2,1,0:T(8,128)(2,1)} %middle_ref.1, bf16[9,16,128]{2,1,0:T(8,128)(2,1)} %last_ref.1, f32[1,16]{1,0:T(1,128)} %bitcast.7), custom_call_target="tpu_custom_call" | custom-call | tf_op jit(solution)/shard_map/pallas_call | solution.py:384
  9.4 0.0 collective-permute-done.4.refs_5_
  9.5 0.0 collective-permute-done.3.refs_4_
  9.5 0.1 collective-permute-done.refs_1_
  9.6 0.0 collective-permute-done.2.refs_3_
  9.6 0.0 collective-permute-done.1.refs_2_
  9.6 0.0 copy-done
  9.6 7.8 %shard_map.84 = f32[1,16,16,128]{3,2,1,0:T(8,128)} custom-call(f32[16,16,128]{2,1,0:T(8,128)S(1)} %copy-done, f32[3,128]{1,0:T(4,128)S(1)} %collective-permute-done.refs_1_, f32[16,16,128]{2,1,0:T(8,128)S(1)} %collective-permute-done.1.refs_2_, f32[16,16,128]{2,1,0:T(8,128)S(1)} %collective-permute-done.2.refs_3_, ...), custom_call_target="tpu_custom_call" | custom-call | tf_op jit(solution)/shard_map/pallas_call | solution.py:402
Async XLA Ops:
  2.0 7.6 %collective-permute-start.2 = (f32[16,16,128]{2,1,0:T(8,128)}, f32[16,16,128]{2,1,0:T(8,128)S(1)}, u32[]{:S(2)}, u32[]{:S(2)}) collective-permute-start(f32[16,16,128]{2,1,0:T(8,128)} %refs_0_), channel_id=1, source_target_pairs={{1,2},{0,3},{2,1},{3,0},{5,6},{4,7},{6,5},{7,4},{9,10},{8,11},{10,... | collective-permute-start | bytes 393224 | tf_op jit(solution)/shard_map/ppermute | solution.py:372
  3.0 6.6 %collective-permute-start.1 = (f32[16,16,128]{2,1,0:T(8,128)}, f32[16,16,128]{2,1,0:T(8,128)S(1)}, u32[]{:S(2)}, u32[]{:S(2)}) collective-permute-start(f32[16,16,128]{2,1,0:T(8,128)} %refs_0_), channel_id=1, source_target_pairs={{0,1},{2,3},{1,0},{3,2},{4,5},{6,7},{5,4},{7,6},{8,9},{10,11},{9,8... | collective-permute-start | bytes 393224 | tf_op jit(solution)/shard_map/ppermute | solution.py:372
  3.6 5.8 %collective-permute-start.4 = (f32[3,128]{1,0:T(4,128)S(1)}, f32[3,128]{1,0:T(4,128)S(1)}, u32[]{:S(2)}, u32[]{:S(2)}) collective-permute-start(f32[3,128]{1,0:T(4,128)S(1)} %shard_map.82), channel_id=1, source_target_pairs={{0,12},{4,8},{8,4},{12,0},{1,13},{5,9},{9,5},{13,1},{2,14},{6,10},... | collective-permute-start | bytes 4616 | tf_op jit(solution)/shard_map/ppermute | solution.py:375
  3.9 5.6 %collective-permute-start.3 = (f32[3,128]{1,0:T(4,128)S(1)}, f32[3,128]{1,0:T(4,128)S(1)}, u32[]{:S(2)}, u32[]{:S(2)}) collective-permute-start(f32[3,128]{1,0:T(4,128)S(1)} %shard_map.82), channel_id=1, source_target_pairs={{0,4},{4,0},{8,12},{12,8},{1,5},{5,1},{9,13},{13,9},{2,6},{6,2},{1... | collective-permute-start | bytes 4616 | tf_op jit(solution)/shard_map/ppermute | solution.py:375
  4.5 5.0 %collective-permute-start = (f32[3,128]{1,0:T(4,128)S(1)}, f32[3,128]{1,0:T(4,128)S(1)}, u32[]{:S(2)}, u32[]{:S(2)}) collective-permute-start(f32[3,128]{1,0:T(4,128)S(1)} %shard_map.82), channel_id=1, source_target_pairs={{0,8},{4,12},{8,0},{12,4},{1,9},{5,13},{9,1},{13,5},{2,10},{6,14},... | collective-permute-start | bytes 4616 | tf_op jit(solution)/shard_map/ppermute | solution.py:375
  8.0 1.6 %copy-start = (f32[16,16,128]{2,1,0:T(8,128)S(1)}, f32[16,16,128]{2,1,0:T(8,128)}, u32[]{:S(2)}) copy-start(f32[16,16,128]{2,1,0:T(8,128)} %refs_0_) | copy-start | bytes 393220

commit v8 on v7

--- a/solution.py
+++ b/solution.py
@@ -335,15 +335,13 @@
                 for r in range(8):
                     out_ref[0, :, 8 * t + r, :] = moved[16 * r : 16 * r + 16]
 
-    for step in range(ITERS):
-
-        @pl.when(time == ITERS - step)
+    for start in range(ITERS):
+
+        @pl.when(time == ITERS - start)
         def _():
-            build_state(HALO - 3 * step)
-
-        @pl.when(time >= ITERS - step)
-        def _():
-            one_step(step)
+            build_state(HALO - 3 * start)
+            for step in range(start, ITERS):
+                one_step(step)
 
     @pl.when(time == 0)
     def _():

time: 17.5 us -> 17.3 us (0.989)
  Pallas kernels: 9.9 us -> 9.7 us
    pallas_call x1, Pallas kernels: 7.77 us -> 7.56 us  [chain(): pl.pallas_call(body, out_shape=shape((1, channels, rows, cols), F32), in_...]
where the time goes in v8:
time: 17.3 us; the launch traced here: 17.2 us
  Pallas kernels  9.7 us (56%)
  starting transfers between devices  5.99 us (35%)
  between operations  1.33 us (8%)
    pallas_call x1, Pallas kernels, chain(): pl.pallas_call(body, out_shape=shape((1, channels, rows, cols), F32), in_...  7.56 us
    ppermute x3, starting transfers between devices, exchanged(): return lax.ppermute(far, 'tm', [(t, t ^ apart) for t in range(tm_size)])  4.39 us
    ppermute x2, starting transfers between devices, swapped(): return lax.ppermute(value, 'space', pairs + [(j, i) for i, j in pairs])  1.61 us
    pallas_call x1, Pallas kernels, chain(): pl.pallas_call(weights_kernel, out_shape=(pltpu.VMEM((4, 256, 256), BF16)...  1.41 us
    pallas_call x1, Pallas kernels, chain(): pl.pallas_call(pack_kernel, out_shape=pltpu.VMEM((3, cols), F32), in_spec...  0.73 us
  transfers between devices with their start and end apart: 5, of which 1 were waited for; matrix products, arithmetic and copies ran while one was open for 0% of the time, Pallas kernels for 8%

profile of v8, /device:TPU:24, one launch (start us, length us, event | category | flops | bytes accessed | tf_op | source)
XLA Modules:
  0.0 17.2 jit_solution(366729074661251986)
XLA Ops:
  1.3 0.7 %shard_map.82 = f32[3,128]{1,0:T(4,128)S(1)} custom-call(f32[1,128]{1,0:T(1,128)} %embed_ref.1, f32[1,1]{1,0:T(1,128)} %bitcast.4.keep_ref, f32[1,1]{1,0:T(1,128)} %bitcast.5.rate_ref), custom_call_target="tpu_custom_call" | custom-call | tf_op jit(solution)/shard_map/pallas_call | solution.py:360
  2.0 0.9 %collective-permute-start.2 = (f32[16,16,128]{2,1,0:T(8,128)}, f32[16,16,128]{2,1,0:T(8,128)S(1)}, u32[]{:S(2)}, u32[]{:S(2)}) collective-permute-start(f32[16,16,128]{2,1,0:T(8,128)} %refs_0_), channel_id=1, source_target_pairs={{1,2},{0,3},{2,1},{3,0},{5,6},{4,7},{6,5},{7,4},{9,10},{8,11},{10,... | collective-permute-start | bytes 393224 | tf_op jit(solution)/shard_map/ppermute | solution.py:370
  3.0 0.7 %collective-permute-start.1 = (f32[16,16,128]{2,1,0:T(8,128)}, f32[16,16,128]{2,1,0:T(8,128)S(1)}, u32[]{:S(2)}, u32[]{:S(2)}) collective-permute-start(f32[16,16,128]{2,1,0:T(8,128)} %refs_0_), channel_id=1, source_target_pairs={{0,1},{2,3},{1,0},{3,2},{4,5},{6,7},{5,4},{7,6},{8,9},{10,11},{9,8... | collective-permute-start | bytes 393224 | tf_op jit(solution)/shard_map/ppermute | solution.py:370
  3.6 0.2 %collective-permute-start.4 = (f32[3,128]{1,0:T(4,128)S(1)}, f32[3,128]{1,0:T(4,128)S(1)}, u32[]{:S(2)}, u32[]{:S(2)}) collective-permute-start(f32[3,128]{1,0:T(4,128)S(1)} %shard_map.82), channel_id=1, source_target_pairs={{0,12},{4,8},{8,4},{12,0},{1,13},{5,9},{9,5},{13,1},{2,14},{6,10},... | collective-permute-start | bytes 4616 | tf_op jit(solution)/shard_map/ppermute | solution.py:373
  3.9 0.7 %collective-permute-start.3 = (f32[3,128]{1,0:T(4,128)S(1)}, f32[3,128]{1,0:T(4,128)S(1)}, u32[]{:S(2)}, u32[]{:S(2)}) collective-permute-start(f32[3,128]{1,0:T(4,128)S(1)} %shard_map.82), channel_id=1, source_target_pairs={{0,4},{4,0},{8,12},{12,8},{1,5},{5,1},{9,13},{13,9},{2,6},{6,2},{1... | collective-permute-start | bytes 4616 | tf_op jit(solution)/shard_map/ppermute | solution.py:373
  4.5 3.5 %collective-permute-start = (f32[3,128]{1,0:T(4,128)S(1)}, f32[3,128]{1,0:T(4,128)S(1)}, u32[]{:S(2)}, u32[]{:S(2)}) collective-permute-start(f32[3,128]{1,0:T(4,128)S(1)} %shard_map.82), channel_id=1, source_target_pairs={{0,8},{4,12},{8,0},{12,4},{1,9},{5,13},{9,1},{13,5},{2,10},{6,14},... | collective-permute-start | bytes 4616 | tf_op jit(solution)/shard_map/ppermute | solution.py:373
  8.0 0.0 copy-start
  8.0 1.4 %shard_map.83 = (bf16[4,256,256]{2,1,0:T(8,128)(2,1)S(1)}, bf16[1536,256]{1,0:T(8,128)(2,1)S(1)}, bf16[4,256,256]{2,1,0:T(8,128)(2,1)S(1)}, f32[1,128]{1,0:T(1,128)S(1)}) custom-call(bf16[9,16,128]{2,1,0:T(8,128)(2,1)} %bitcast.6, bf16[9,128,128]{2,1,0:T(8,128)(2,1)} %middle_ref.1, bf16[9,16,128]{2,1,0:T(8,128)(2,1)} %last_ref.1, f32[1,16]{1,0:T(1,128)} %bitcast.7), custom_call_target="tpu_custom_call" | custom-call | tf_op jit(solution)/shard_map/pallas_call | solution.py:382
  9.4 0.0 collective-permute-done.4.refs_5_
  9.5 0.0 collective-permute-done.3.refs_4_
  9.5 0.1 collective-permute-done.refs_1_
  9.6 0.0 collective-permute-done.2.refs_3_
  9.6 0.0 collective-permute-done.1.refs_2_
  9.6 0.0 copy-done
  9.6 7.6 %shard_map.84 = f32[1,16,16,128]{3,2,1,0:T(8,128)} custom-call(f32[16,16,128]{2,1,0:T(8,128)S(1)} %copy-done, f32[3,128]{1,0:T(4,128)S(1)} %collective-permute-done.refs_1_, f32[16,16,128]{2,1,0:T(8,128)S(1)} %collective-permute-done.1.refs_2_, f32[16,16,128]{2,1,0:T(8,128)S(1)} %collective-permute-done.2.refs_3_, ...), custom_call_target="tpu_custom_call" | custom-call | tf_op jit(solution)/shard_map/pallas_call | solution.py:400
Async XLA Ops:
  2.0 7.6 %collective-permute-start.2 = (f32[16,16,128]{2,1,0:T(8,128)}, f32[16,16,128]{2,1,0:T(8,128)S(1)}, u32[]{:S(2)}, u32[]{:S(2)}) collective-permute-start(f32[16,16,128]{2,1,0:T(8,128)} %refs_0_), channel_id=1, source_target_pairs={{1,2},{0,3},{2,1},{3,0},{5,6},{4,7},{6,5},{7,4},{9,10},{8,11},{10,... | collective-permute-start | bytes 393224 | tf_op jit(solution)/shard_map/ppermute | solution.py:370
  3.0 6.6 %collective-permute-start.1 = (f32[16,16,128]{2,1,0:T(8,128)}, f32[16,16,128]{2,1,0:T(8,128)S(1)}, u32[]{:S(2)}, u32[]{:S(2)}) collective-permute-start(f32[16,16,128]{2,1,0:T(8,128)} %refs_0_), channel_id=1, source_target_pairs={{0,1},{2,3},{1,0},{3,2},{4,5},{6,7},{5,4},{7,6},{8,9},{10,11},{9,8... | collective-permute-start | bytes 393224 | tf_op jit(solution)/shard_map/ppermute | solution.py:370
  3.6 5.8 %collective-permute-start.4 = (f32[3,128]{1,0:T(4,128)S(1)}, f32[3,128]{1,0:T(4,128)S(1)}, u32[]{:S(2)}, u32[]{:S(2)}) collective-permute-start(f32[3,128]{1,0:T(4,128)S(1)} %shard_map.82), channel_id=1, source_target_pairs={{0,12},{4,8},{8,4},{12,0},{1,13},{5,9},{9,5},{13,1},{2,14},{6,10},... | collective-permute-start | bytes 4616 | tf_op jit(solution)/shard_map/ppermute | solution.py:373
  3.9 5.6 %collective-permute-start.3 = (f32[3,128]{1,0:T(4,128)S(1)}, f32[3,128]{1,0:T(4,128)S(1)}, u32[]{:S(2)}, u32[]{:S(2)}) collective-permute-start(f32[3,128]{1,0:T(4,128)S(1)} %shard_map.82), channel_id=1, source_target_pairs={{0,4},{4,0},{8,12},{12,8},{1,5},{5,1},{9,13},{13,9},{2,6},{6,2},{1... | collective-permute-start | bytes 4616 | tf_op jit(solution)/shard_map/ppermute | solution.py:373
  4.5 5.0 %collective-permute-start = (f32[3,128]{1,0:T(4,128)S(1)}, f32[3,128]{1,0:T(4,128)S(1)}, u32[]{:S(2)}, u32[]{:S(2)}) collective-permute-start(f32[3,128]{1,0:T(4,128)S(1)} %shard_map.82), channel_id=1, source_target_pairs={{0,8},{4,12},{8,0},{12,4},{1,9},{5,13},{9,1},{13,5},{2,10},{6,14},... | collective-permute-start | bytes 4616 | tf_op jit(solution)/shard_map/ppermute | solution.py:373
  8.0 1.6 %copy-start = (f32[16,16,128]{2,1,0:T(8,128)S(1)}, f32[16,16,128]{2,1,0:T(8,128)}, u32[]{:S(2)}) copy-start(f32[16,16,128]{2,1,0:T(8,128)} %refs_0_) | copy-start | bytes 393220

commit v9 on v8

--- a/solution.py
+++ b/solution.py
@@ -106,7 +106,7 @@
     zero = jnp.zeros((128, 128), BF16)
     for tap in range(9):
         a, b = divmod(tap, 3)
-        block = (middle_ref[tap].astype(F32).T * 0.5).astype(BF16)
+        block = middle_ref[tap].T * BF16(0.5)
         for out in range(2):
             wm_ref[pl.ds(512 * b + 128 * (out + a), 128), pl.ds(128 * out, 128)] = block
     for b in range(3):
@@ -121,10 +121,10 @@
                     a = row + 2 - k % 4
                     b = 2 if part else k // 4
                     if 0 <= a < 3 and not (part and k >= 4):
-                        parts.append(last_ref[3 * a + b].astype(F32))
+                        parts.append(last_ref[3 * a + b])
                     else:
-                        parts.append(jnp.zeros((16, 128), F32))
-                block = jnp.concatenate(parts, axis=0).T.astype(BF16)
+                        parts.append(none)
+                block = jnp.concatenate(parts, axis=0).T
                 w3_ref[place, pl.ds(128 * row, 128), pl.ds(128 * part, 128)] = block
 
 

time: 17.3 us -> 17.3 us (level)
  no operation moved by 1% of the time
where the time goes in v9:
time: 17.3 us; the launch traced here: 17.2 us
  Pallas kernels  9.61 us (56%)
  starting transfers between devices  5.99 us (35%)
  between operations  1.33 us (8%)
  waiting for transfers between devices  0.22 us (1%)
    pallas_call x1, Pallas kernels, chain(): pl.pallas_call(body, out_shape=shape((1, channels, rows, cols), F32), in_...  7.56 us
    ppermute x3, starting transfers between devices, exchanged(): return lax.ppermute(far, 'tm', [(t, t ^ apart) for t in range(tm_size)])  4.39 us
    ppermute x2, starting transfers between devices, swapped(): return lax.ppermute(value, 'space', pairs + [(j, i) for i, j in pairs])  1.61 us
    pallas_call x1, Pallas kernels, chain(): pl.pallas_call(weights_kernel, out_shape=(pltpu.VMEM((4, 256, 256), BF16)...  1.32 us
    pallas_call x1, Pallas kernels, chain(): pl.pallas_call(pack_kernel, out_shape=pltpu.VMEM((3, cols), F32), in_spec...  0.73 us
  transfers between devices with their start and end apart: 5, of which 1 were waited for; matrix products, arithmetic and copies ran while one was open for 0% of the time, Pallas kernels for 8%

profile of v9, /device:TPU:24, one launch (start us, length us, event | category | flops | bytes accessed | tf_op | source)
XLA Modules:
  0.0 17.2 jit_solution(1500170331334571749)
XLA Ops:
  1.3 0.7 %shard_map.82 = f32[3,128]{1,0:T(4,128)S(1)} custom-call(f32[1,128]{1,0:T(1,128)} %embed_ref.1, f32[1,1]{1,0:T(1,128)} %bitcast.4.keep_ref, f32[1,1]{1,0:T(1,128)} %bitcast.5.rate_ref), custom_call_target="tpu_custom_call" | custom-call | tf_op jit(solution)/shard_map/pallas_call | solution.py:360
  2.0 0.9 %collective-permute-start.2 = (f32[16,16,128]{2,1,0:T(8,128)}, f32[16,16,128]{2,1,0:T(8,128)S(1)}, u32[]{:S(2)}, u32[]{:S(2)}) collective-permute-start(f32[16,16,128]{2,1,0:T(8,128)} %refs_0_), channel_id=1, source_target_pairs={{1,2},{0,3},{2,1},{3,0},{5,6},{4,7},{6,5},{7,4},{9,10},{8,11},{10,... | collective-permute-start | bytes 393224 | tf_op jit(solution)/shard_map/ppermute | solution.py:370
  3.0 0.7 %collective-permute-start.1 = (f32[16,16,128]{2,1,0:T(8,128)}, f32[16,16,128]{2,1,0:T(8,128)S(1)}, u32[]{:S(2)}, u32[]{:S(2)}) collective-permute-start(f32[16,16,128]{2,1,0:T(8,128)} %refs_0_), channel_id=1, source_target_pairs={{0,1},{2,3},{1,0},{3,2},{4,5},{6,7},{5,4},{7,6},{8,9},{10,11},{9,8... | collective-permute-start | bytes 393224 | tf_op jit(solution)/shard_map/ppermute | solution.py:370
  3.6 0.2 %collective-permute-start.4 = (f32[3,128]{1,0:T(4,128)S(1)}, f32[3,128]{1,0:T(4,128)S(1)}, u32[]{:S(2)}, u32[]{:S(2)}) collective-permute-start(f32[3,128]{1,0:T(4,128)S(1)} %shard_map.82), channel_id=1, source_target_pairs={{0,12},{4,8},{8,4},{12,0},{1,13},{5,9},{9,5},{13,1},{2,14},{6,10},... | collective-permute-start | bytes 4616 | tf_op jit(solution)/shard_map/ppermute | solution.py:373
  3.9 0.7 %collective-permute-start.3 = (f32[3,128]{1,0:T(4,128)S(1)}, f32[3,128]{1,0:T(4,128)S(1)}, u32[]{:S(2)}, u32[]{:S(2)}) collective-permute-start(f32[3,128]{1,0:T(4,128)S(1)} %shard_map.82), channel_id=1, source_target_pairs={{0,4},{4,0},{8,12},{12,8},{1,5},{5,1},{9,13},{13,9},{2,6},{6,2},{1... | collective-permute-start | bytes 4616 | tf_op jit(solution)/shard_map/ppermute | solution.py:373
  4.5 3.5 %collective-permute-start = (f32[3,128]{1,0:T(4,128)S(1)}, f32[3,128]{1,0:T(4,128)S(1)}, u32[]{:S(2)}, u32[]{:S(2)}) collective-permute-start(f32[3,128]{1,0:T(4,128)S(1)} %shard_map.82), channel_id=1, source_target_pairs={{0,8},{4,12},{8,0},{12,4},{1,9},{5,13},{9,1},{13,5},{2,10},{6,14},... | collective-permute-start | bytes 4616 | tf_op jit(solution)/shard_map/ppermute | solution.py:373
  8.0 0.0 copy-start
  8.0 1.3 %shard_map.83 = (bf16[4,256,256]{2,1,0:T(8,128)(2,1)S(1)}, bf16[1536,256]{1,0:T(8,128)(2,1)S(1)}, bf16[4,256,256]{2,1,0:T(8,128)(2,1)S(1)}, f32[1,128]{1,0:T(1,128)S(1)}) custom-call(bf16[9,16,128]{2,1,0:T(8,128)(2,1)} %bitcast.6, bf16[9,128,128]{2,1,0:T(8,128)(2,1)} %middle_ref.1, bf16[9,16,128]{2,1,0:T(8,128)(2,1)} %last_ref.1, f32[1,16]{1,0:T(1,128)} %bitcast.7), custom_call_target="tpu_custom_call" | custom-call | tf_op jit(solution)/shard_map/pallas_call | solution.py:382
  9.4 0.0 collective-permute-done.4.refs_5_
  9.4 0.0 collective-permute-done.3.refs_4_
  9.4 0.2 %collective-permute-done.refs_1_ = f32[3,128]{1,0:T(4,128)S(1)} collective-permute-done((f32[3,128]{1,0:T(4,128)S(1)}, f32[3,128]{1,0:T(4,128)S(1)}, u32[]{:S(2)}, u32[]{:S(2)}) %collective-permute-start) | collective-permute-done | bytes 1568 | tf_op jit(solution)/shard_map/ppermute | solution.py:373
  9.6 0.0 collective-permute-done.2.refs_3_
  9.6 0.0 collective-permute-done.1.refs_2_
  9.6 0.0 copy-done
  9.6 7.6 %shard_map.84 = f32[1,16,16,128]{3,2,1,0:T(8,128)} custom-call(f32[16,16,128]{2,1,0:T(8,128)S(1)} %copy-done, f32[3,128]{1,0:T(4,128)S(1)} %collective-permute-done.refs_1_, f32[16,16,128]{2,1,0:T(8,128)S(1)} %collective-permute-done.1.refs_2_, f32[16,16,128]{2,1,0:T(8,128)S(1)} %collective-permute-done.2.refs_3_, ...), custom_call_target="tpu_custom_call" | custom-call | tf_op jit(solution)/shard_map/pallas_call | solution.py:400
Async XLA Ops:
  2.0 7.6 %collective-permute-start.2 = (f32[16,16,128]{2,1,0:T(8,128)}, f32[16,16,128]{2,1,0:T(8,128)S(1)}, u32[]{:S(2)}, u32[]{:S(2)}) collective-permute-start(f32[16,16,128]{2,1,0:T(8,128)} %refs_0_), channel_id=1, source_target_pairs={{1,2},{0,3},{2,1},{3,0},{5,6},{4,7},{6,5},{7,4},{9,10},{8,11},{10,... | collective-permute-start | bytes 393224 | tf_op jit(solution)/shard_map/ppermute | solution.py:370
  3.0 6.6 %collective-permute-start.1 = (f32[16,16,128]{2,1,0:T(8,128)}, f32[16,16,128]{2,1,0:T(8,128)S(1)}, u32[]{:S(2)}, u32[]{:S(2)}) collective-permute-start(f32[16,16,128]{2,1,0:T(8,128)} %refs_0_), channel_id=1, source_target_pairs={{0,1},{2,3},{1,0},{3,2},{4,5},{6,7},{5,4},{7,6},{8,9},{10,11},{9,8... | collective-permute-start | bytes 393224 | tf_op jit(solution)/shard_map/ppermute | solution.py:370
  3.6 5.7 %collective-permute-start.4 = (f32[3,128]{1,0:T(4,128)S(1)}, f32[3,128]{1,0:T(4,128)S(1)}, u32[]{:S(2)}, u32[]{:S(2)}) collective-permute-start(f32[3,128]{1,0:T(4,128)S(1)} %shard_map.82), channel_id=1, source_target_pairs={{0,12},{4,8},{8,4},{12,0},{1,13},{5,9},{9,5},{13,1},{2,14},{6,10},... | collective-permute-start | bytes 4616 | tf_op jit(solution)/shard_map/ppermute | solution.py:373
  3.9 5.5 %collective-permute-start.3 = (f32[3,128]{1,0:T(4,128)S(1)}, f32[3,128]{1,0:T(4,128)S(1)}, u32[]{:S(2)}, u32[]{:S(2)}) collective-permute-start(f32[3,128]{1,0:T(4,128)S(1)} %shard_map.82), channel_id=1, source_target_pairs={{0,4},{4,0},{8,12},{12,8},{1,5},{5,1},{9,13},{13,9},{2,6},{6,2},{1... | collective-permute-start | bytes 4616 | tf_op jit(solution)/shard_map/ppermute | solution.py:373
  4.5 5.0 %collective-permute-start = (f32[3,128]{1,0:T(4,128)S(1)}, f32[3,128]{1,0:T(4,128)S(1)}, u32[]{:S(2)}, u32[]{:S(2)}) collective-permute-start(f32[3,128]{1,0:T(4,128)S(1)} %shard_map.82), channel_id=1, source_target_pairs={{0,8},{4,12},{8,0},{12,4},{1,9},{5,13},{9,1},{13,5},{2,10},{6,14},... | collective-permute-start | bytes 4616 | tf_op jit(solution)/shard_map/ppermute | solution.py:373
  8.0 1.6 %copy-start = (f32[16,16,128]{2,1,0:T(8,128)S(1)}, f32[16,16,128]{2,1,0:T(8,128)}, u32[]{:S(2)}) copy-start(f32[16,16,128]{2,1,0:T(8,128)} %refs_0_) | copy-start | bytes 393220

commit v10 on v8

--- a/solution.py
+++ b/solution.py
@@ -207,12 +207,12 @@
                 else:
                     parts.append(jnp.zeros((16, COLS), F32))
             block = jnp.concatenate(parts, axis=0)
-            moved = None
-            for piece in split3(block):
-                part = lax.dot_general(
-                    order, piece, (((1,), (1,)), ((), ())), preferred_element_type=F32
-                )
-                moved = part if moved is None else moved + part
+            moved = lax.dot_general(
+                jnp.concatenate([order] * 3, axis=1),
+                jnp.concatenate(split3(block), axis=1),
+                (((1,), (1,)), ((), ())),
+                preferred_element_type=F32,
+            )
             state_ref[t] = moved * lane_scale(t, halo)
 
     bias = bias_ref[...]
@@ -328,10 +328,11 @@
                 state_ref[t] = new * lane_scale(t, halo - 3)
             else:
                 turned = new.T
-                moved = None
-                for piece in split3(turned):
-                    part = jnp.dot(piece, order, preferred_element_type=F32)
-                    moved = part if moved is None else moved + part
+                moved = jnp.dot(
+                    jnp.concatenate(split3(turned), axis=1),
+                    jnp.concatenate([order] * 3, axis=0),
+                    preferred_element_type=F32,
+                )
                 for r in range(8):
                     out_ref[0, :, 8 * t + r, :] = moved[16 * r : 16 * r + 16]
 

time: 17.3 us -> 17.2 us (level)
  no operation moved by 1% of the time
where the time goes in v10:
time: 17.2 us; the launch traced here: 17 us
  Pallas kernels  9.59 us (56%)
  starting transfers between devices  5.99 us (35%)
  between operations  1.33 us (8%)
    pallas_call x1, Pallas kernels, chain(): pl.pallas_call(body, out_shape=shape((1, channels, rows, cols), F32), in_...  7.45 us
    ppermute x3, starting transfers between devices, exchanged(): return lax.ppermute(far, 'tm', [(t, t ^ apart) for t in range(tm_size)])  4.39 us
    ppermute x2, starting transfers between devices, swapped(): return lax.ppermute(value, 'space', pairs + [(j, i) for i, j in pairs])  1.61 us
    pallas_call x1, Pallas kernels, chain(): pl.pallas_call(weights_kernel, out_shape=(pltpu.VMEM((4, 256, 256), BF16)...  1.41 us
    pallas_call x1, Pallas kernels, chain(): pl.pallas_call(pack_kernel, out_shape=pltpu.VMEM((3, cols), F32), in_spec...  0.73 us
  transfers between devices with their start and end apart: 5, of which 1 were waited for; matrix products, arithmetic and copies ran while one was open for 0% of the time, Pallas kernels for 8%

profile of v10, /device:TPU:24, one launch (start us, length us, event | category | flops | bytes accessed | tf_op | source)
XLA Modules:
  0.0 17.0 jit_solution(11206996315947199435)
XLA Ops:
  1.3 0.7 %shard_map.82 = f32[3,128]{1,0:T(4,128)S(1)} custom-call(f32[1,128]{1,0:T(1,128)} %embed_ref.1, f32[1,1]{1,0:T(1,128)} %bitcast.4.keep_ref, f32[1,1]{1,0:T(1,128)} %bitcast.5.rate_ref), custom_call_target="tpu_custom_call" | custom-call | tf_op jit(solution)/shard_map/pallas_call | solution.py:361
  2.0 0.9 %collective-permute-start.2 = (f32[16,16,128]{2,1,0:T(8,128)}, f32[16,16,128]{2,1,0:T(8,128)S(1)}, u32[]{:S(2)}, u32[]{:S(2)}) collective-permute-start(f32[16,16,128]{2,1,0:T(8,128)} %refs_0_), channel_id=1, source_target_pairs={{1,2},{0,3},{2,1},{3,0},{5,6},{4,7},{6,5},{7,4},{9,10},{8,11},{10,... | collective-permute-start | bytes 393224 | tf_op jit(solution)/shard_map/ppermute | solution.py:371
  3.0 0.7 %collective-permute-start.1 = (f32[16,16,128]{2,1,0:T(8,128)}, f32[16,16,128]{2,1,0:T(8,128)S(1)}, u32[]{:S(2)}, u32[]{:S(2)}) collective-permute-start(f32[16,16,128]{2,1,0:T(8,128)} %refs_0_), channel_id=1, source_target_pairs={{0,1},{2,3},{1,0},{3,2},{4,5},{6,7},{5,4},{7,6},{8,9},{10,11},{9,8... | collective-permute-start | bytes 393224 | tf_op jit(solution)/shard_map/ppermute | solution.py:371
  3.6 0.2 %collective-permute-start.4 = (f32[3,128]{1,0:T(4,128)S(1)}, f32[3,128]{1,0:T(4,128)S(1)}, u32[]{:S(2)}, u32[]{:S(2)}) collective-permute-start(f32[3,128]{1,0:T(4,128)S(1)} %shard_map.82), channel_id=1, source_target_pairs={{0,12},{4,8},{8,4},{12,0},{1,13},{5,9},{9,5},{13,1},{2,14},{6,10},... | collective-permute-start | bytes 4616 | tf_op jit(solution)/shard_map/ppermute | solution.py:374
  3.9 0.7 %collective-permute-start.3 = (f32[3,128]{1,0:T(4,128)S(1)}, f32[3,128]{1,0:T(4,128)S(1)}, u32[]{:S(2)}, u32[]{:S(2)}) collective-permute-start(f32[3,128]{1,0:T(4,128)S(1)} %shard_map.82), channel_id=1, source_target_pairs={{0,4},{4,0},{8,12},{12,8},{1,5},{5,1},{9,13},{13,9},{2,6},{6,2},{1... | collective-permute-start | bytes 4616 | tf_op jit(solution)/shard_map/ppermute | solution.py:374
  4.5 3.5 %collective-permute-start = (f32[3,128]{1,0:T(4,128)S(1)}, f32[3,128]{1,0:T(4,128)S(1)}, u32[]{:S(2)}, u32[]{:S(2)}) collective-permute-start(f32[3,128]{1,0:T(4,128)S(1)} %shard_map.82), channel_id=1, source_target_pairs={{0,8},{4,12},{8,0},{12,4},{1,9},{5,13},{9,1},{13,5},{2,10},{6,14},... | collective-permute-start | bytes 4616 | tf_op jit(solution)/shard_map/ppermute | solution.py:374
  8.0 0.0 copy-start
  8.0 1.4 %shard_map.83 = (bf16[4,256,256]{2,1,0:T(8,128)(2,1)S(1)}, bf16[1536,256]{1,0:T(8,128)(2,1)S(1)}, bf16[4,256,256]{2,1,0:T(8,128)(2,1)S(1)}, f32[1,128]{1,0:T(1,128)S(1)}) custom-call(bf16[9,16,128]{2,1,0:T(8,128)(2,1)} %bitcast.6, bf16[9,128,128]{2,1,0:T(8,128)(2,1)} %middle_ref.1, bf16[9,16,128]{2,1,0:T(8,128)(2,1)} %last_ref.1, f32[1,16]{1,0:T(1,128)} %bitcast.7), custom_call_target="tpu_custom_call" | custom-call | tf_op jit(solution)/shard_map/pallas_call | solution.py:383
  9.4 0.0 collective-permute-done.4.refs_5_
  9.5 0.0 collective-permute-done.3.refs_4_
  9.5 0.1 collective-permute-done.refs_1_
  9.6 0.0 collective-permute-done.2.refs_3_
  9.6 0.0 collective-permute-done.1.refs_2_
  9.6 0.0 copy-done
  9.6 7.5 %shard_map.84 = f32[1,16,16,128]{3,2,1,0:T(8,128)} custom-call(f32[16,16,128]{2,1,0:T(8,128)S(1)} %copy-done, f32[3,128]{1,0:T(4,128)S(1)} %collective-permute-done.refs_1_, f32[16,16,128]{2,1,0:T(8,128)S(1)} %collective-permute-done.1.refs_2_, f32[16,16,128]{2,1,0:T(8,128)S(1)} %collective-permute-done.2.refs_3_, ...), custom_call_target="tpu_custom_call" | custom-call | tf_op jit(solution)/shard_map/pallas_call | solution.py:401
Async XLA Ops:
  2.0 7.6 %collective-permute-start.2 = (f32[16,16,128]{2,1,0:T(8,128)}, f32[16,16,128]{2,1,0:T(8,128)S(1)}, u32[]{:S(2)}, u32[]{:S(2)}) collective-permute-start(f32[16,16,128]{2,1,0:T(8,128)} %refs_0_), channel_id=1, source_target_pairs={{1,2},{0,3},{2,1},{3,0},{5,6},{4,7},{6,5},{7,4},{9,10},{8,11},{10,... | collective-permute-start | bytes 393224 | tf_op jit(solution)/shard_map/ppermute | solution.py:371
  3.0 6.6 %collective-permute-start.1 = (f32[16,16,128]{2,1,0:T(8,128)}, f32[16,16,128]{2,1,0:T(8,128)S(1)}, u32[]{:S(2)}, u32[]{:S(2)}) collective-permute-start(f32[16,16,128]{2,1,0:T(8,128)} %refs_0_), channel_id=1, source_target_pairs={{0,1},{2,3},{1,0},{3,2},{4,5},{6,7},{5,4},{7,6},{8,9},{10,11},{9,8... | collective-permute-start | bytes 393224 | tf_op jit(solution)/shard_map/ppermute | solution.py:371
  3.6 5.8 %collective-permute-start.4 = (f32[3,128]{1,0:T(4,128)S(1)}, f32[3,128]{1,0:T(4,128)S(1)}, u32[]{:S(2)}, u32[]{:S(2)}) collective-permute-start(f32[3,128]{1,0:T(4,128)S(1)} %shard_map.82), channel_id=1, source_target_pairs={{0,12},{4,8},{8,4},{12,0},{1,13},{5,9},{9,5},{13,1},{2,14},{6,10},... | collective-permute-start | bytes 4616 | tf_op jit(solution)/shard_map/ppermute | solution.py:374
  3.9 5.6 %collective-permute-start.3 = (f32[3,128]{1,0:T(4,128)S(1)}, f32[3,128]{1,0:T(4,128)S(1)}, u32[]{:S(2)}, u32[]{:S(2)}) collective-permute-start(f32[3,128]{1,0:T(4,128)S(1)} %shard_map.82), channel_id=1, source_target_pairs={{0,4},{4,0},{8,12},{12,8},{1,5},{5,1},{9,13},{13,9},{2,6},{6,2},{1... | collective-permute-start | bytes 4616 | tf_op jit(solution)/shard_map/ppermute | solution.py:374
  4.5 5.0 %collective-permute-start = (f32[3,128]{1,0:T(4,128)S(1)}, f32[3,128]{1,0:T(4,128)S(1)}, u32[]{:S(2)}, u32[]{:S(2)}) collective-permute-start(f32[3,128]{1,0:T(4,128)S(1)} %shard_map.82), channel_id=1, source_target_pairs={{0,8},{4,12},{8,0},{12,4},{1,9},{5,13},{9,1},{13,5},{2,10},{6,14},... | collective-permute-start | bytes 4616 | tf_op jit(solution)/shard_map/ppermute | solution.py:374
  8.0 1.6 %copy-start = (f32[16,16,128]{2,1,0:T(8,128)S(1)}, f32[16,16,128]{2,1,0:T(8,128)}, u32[]{:S(2)}) copy-start(f32[16,16,128]{2,1,0:T(8,128)} %refs_0_) | copy-start | bytes 393220
